TPU v7x, 128 devices: a whole 4x4x4 slice. The times are simulated.
128 devices in a mesh: pts: 16 (over z, y), hrs: 8 (over x, core).
Axes of the slice: x: 4, y: 4, z: 4, core: 2. Of those that a mesh axis runs over, the one named last changes fastest.
Arguments:
- fields: float32 [512, 262144], P(('pts', 'hrs')), may hold values from -2000 to 2000, as said below
- probes: float32 [256, 512], replicated, may hold values from -0.25 to 0.25
Outputs:
- basis_rows: float32 [256, 262144], P(None, ('pts', 'hrs'))
- coeffs: float32 [256, 512], replicated
Inputs may be any that keep to these rules, and one draw needn't show every extreme that they name: `fields`: every hour and every grid point carries its own scale, and the values are real-valued and never all zero.
All inputs are finite; a program needn't handle non-finite values.
Results may differ from a plain program's by a relative error of at most 0.00017.
Values sent between devices are 32-bit elements; how exact they have to be, the bound alone decides.
No kernel may reach another device: no remote copies, remote signals or barrier semaphores. Data moves between devices by JAX's collectives and lax.ppermute only.
A program may use at most 64 MiB of HBM per device.

v0:
```python
import jax
import jax.numpy as jnp
from jax import lax
from jax.sharding import PartitionSpec as P

highest = lax.Precision.HIGHEST


def contract_last(left, right):
    return lax.dot_general(
        left, right, (((1,), (1,)), ((), ())), precision=highest, preferred_element_type=jnp.float32
    )


def on_device(fields, probes):
    n_pts = lax.axis_size("pts")
    n_hrs = lax.axis_size("hrs")
    panels = lax.all_to_all(fields, ("pts", "hrs"), split_axis=1, concat_axis=0, tiled=True)
    n_points = panels.shape[1] * n_pts * n_hrs
    sketched = jnp.dot(probes, panels, precision=highest, preferred_element_type=jnp.float32)
    local_gram = contract_last(sketched, sketched) / n_points
    gram_sum = lax.psum(local_gram, ("pts", "hrs"))
    factor = jnp.linalg.cholesky(gram_sum)
    basis_rows = lax.linalg.triangular_solve(factor, sketched, left_side=True, lower=True)
    coeffs = lax.psum(contract_last(basis_rows, panels) / n_points, ("pts", "hrs"))
    return (basis_rows, coeffs)


def solution(mesh):
    return jax.shard_map(
        on_device,
        mesh=mesh,
        in_specs=(P(("pts", "hrs"), None), P()),
        out_specs=(P(None, ("pts", "hrs")), P()),
        check_vma=False,
    )
```

profile of v0, /device:TPU:1, one launch (start us, length us, event | category | flops | bytes accessed | tf_op | source)
XLA Modules:
  0.0 445.6 jit_solution(2200279935162737825)
XLA Ops:
  7.2 0.0 copy-start
  7.2 0.0 all-reduce.4.cloned.1.call-start
  7.2 64.6 %all_to_all.19 = f32[4,128,2048]{2,0,1:T(4,128)} all-to-all(f32[4,128,2048]{2,0,1:T(4,128)} %bitcast.40), channel_id=1, replica_groups=mesh['pts'=16,'hrs'=8] {'pts','hrs'}, dimensions={1} | all-to-all | bytes 8388608 | tf_op jit(solution)/shard_map/all_to_all | solution.py:18
  71.8 5.3 %all_to_all.17 = f32[512,2048]{1,0:T(8,128)} reshape(f32[128,4,2048]{2,1,0:T(4,128)} %bitcast.39) | data formatting | bytes 8388608 | tf_op jit(solution)/shard_map/all_to_all | solution.py:18
  77.1 0.0 copy-done
  77.1 5.4 %fusion.9 = f32[256,2048]{1,0:T(8,128)S(1)} fusion(f32[256,512]{1,0:T(8,128)S(1)} %copy-done, f32[512,2048]{1,0:T(8,128)} %all_to_all.17), kind=kOutput, calls=%fused_computation.31 | convolution fusion | flops 3221225472 | bytes 6815744 | tf_op jit(solution)/shard_map/dot_general | solution.py:20
  82.6 2.6 convolution_multiply_fusion.1
  85.1 0.0 all-reduce.4.cloned.1.call-update
  85.1 0.2 all-reduce.6.cloned.1.call-start
  85.4 137.0 %all-reduce.4.cloned.1.call-done = f32[256,256]{0,1:T(8,128)} async-done(((f32[256,256]{0,1:T(8,128)}), f32[256,256]{0,1:T(8,128)}) %all-reduce.4.cloned.1.call-update) | async-done | bytes 262160 | tf_op jit(solution)/shard_map/psum | solution.py:22
  222.4 1.1 copy.8
  223.5 1.0 fusion.2
  224.5 11.7 %cholesky.50 = f32[128,128]{1,0:T(8,128)S(1)} custom-call(f32[128,128]{1,0:T(8,128)S(1)} %cholesky.118), custom_call_target="Cholesky" | custom-call | tf_op jit(solution)/shard_map/jit(cholesky)/cholesky | solution.py:23
  236.2 9.8 %custom-call.14 = f32[1,128,128]{1,2,0:T(8,128)S(1)} custom-call(f32[1,128,128]{2,1,0:T(8,128)S(1)} %get-tuple-element.23), custom_call_target="InvertDiagBlocksLowerTriangular" | custom-call | tf_op jit(solution)/shard_map/jit(cholesky)/cholesky | solution.py:23
  246.1 0.2 constant_dynamic-update-slice_fusion.1
  246.3 0.3 convolution_subtract_fusion.1
  246.6 11.7 %cholesky.105 = f32[128,128]{1,0:T(8,128)S(1)} custom-call(f32[128,128]{1,0:T(8,128)S(1)} %convolution_subtract_fusion.1), custom_call_target="Cholesky" | custom-call | tf_op jit(solution)/shard_map/jit(cholesky)/cholesky | solution.py:23
  258.3 0.7 compare_reduce_fusion
  260.3 0.1 triangular_solve.57
  260.4 4.1 while.1
  260.5 0.6 fusion.21
  261.1 1.4 bitcast_dynamic-update-slice_fusion.2
  262.5 0.6 fusion.21
  263.1 1.4 bitcast_dynamic-update-slice_fusion.2
  264.5 19.7 %custom-call.15 = f32[2,128,128]{1,2,0:T(8,128)S(1)} custom-call(f32[2,128,128]{2,1,0:T(8,128)S(1)} %get-tuple-element.9), custom_call_target="InvertDiagBlocksLowerTriangular" | custom-call | tf_op jit(solution)/shard_map/triangular_solve | solution.py:24
  284.1 1.1 fusion
  285.2 1.0 convolution_subtract_fusion
  286.2 1.1 fusion.4
  287.3 0.0 copy-start.1
  287.3 0.1 pad_maximum_fusion
  287.4 2.0 copy-done.1
  289.5 0.0 copy-start.2
  289.5 4.5 %convolution_multiply_fusion = f32[256,512]{1,0:T(8,128)} fusion(f32[256,2048]{1,0:T(8,128)S(1)} %pad_maximum_fusion, f32[512,2048]{1,0:T(8,128)S(1)} %copy-done.1), kind=kOutput, calls=%fused_computation.4 | convolution fusion | flops 3221356544 | bytes 6815744 | tf_op jit(solution)/shard_map/dot_general | solution.py:10
  294.0 0.0 copy-done.2
  294.0 0.0 all-reduce.6.cloned.1.call-update
  294.0 142.8 %all-reduce.6.cloned.1.call-done = f32[256,512]{1,0:T(8,128)} async-done(((f32[256,512]{1,0:T(8,128)}), f32[256,512]{1,0:T(8,128)}) %all-reduce.6.cloned.1.call-update) | async-done | bytes 524304 | tf_op jit(solution)/shard_map/psum | solution.py:25
  436.9 1.9 copy.23
  (9 shorter events, 0.1 us)
Async XLA Ops:
  7.2 70.0 %copy-start = (f32[256,512]{1,0:T(8,128)S(1)}, f32[256,512]{1,0:T(8,128)}, u32[]{:S(2)}) copy-start(f32[256,512]{1,0:T(8,128)} %param.3) | copy-start | bytes 1572868
  7.2 215.2 %all-reduce.4.cloned.1.call-start = ((), (), s32[]{:S(2)}) async-start(), calls=%async_computation.1 | async-start | bytes 524288 | tf_op jit(solution)/shard_map/psum | solution.py:22
  85.1 351.7 %all-reduce.6.cloned.1.call-start = ((), (), s32[]{:S(2)}) async-start(), calls=%async_computation.2 | async-start | bytes 1048576 | tf_op jit(solution)/shard_map/psum | solution.py:25
  287.3 2.2 copy-start.1
  289.5 4.5 %copy-start.2 = (f32[256,2048]{1,0:T(8,128)}, f32[256,2048]{1,0:T(8,128)S(1)}, u32[]{:S(2)}) copy-start(f32[256,2048]{1,0:T(8,128)S(1)} %pad_maximum_fusion) | copy-start | bytes 6291460
Sparse Core Ops, SparseCore 0:
  85.3 137.0 all-reduce.3
  294.1 142.6 all-reduce.5
where the time goes:
time: 446 us
  waiting for transfers between devices  280 us (63%)
  blocking collectives  64.6 us (14%)
  other arithmetic  54.8 us (12%)
  matrix products  16.1 us (4%)
  between operations  15.4 us (3%)
  local copies, waits for them, and re-layouts  14.3 us (3%)
    psum x1, waiting for transfers between devices, on_device(): lax.psum(contract_last(basis_rows, panels) / n_points, ('pts', 'hrs'))  143 us
    psum x1, waiting for transfers between devices, on_device(): gram_sum = lax.psum(local_gram, ('pts', 'hrs'))  137 us
    all_to_all x1, blocking collectives, on_device(): lax.all_to_all(fields, ('pts', 'hrs'), split_axis=1, concat_axis=0, tiled...  64.6 us
    another operation x6, other arithmetic, on_device(): factor = jnp.linalg.cholesky(gram_sum)  34 us
    another operation x4, other arithmetic, on_device(): lax.linalg.triangular_solve(factor, sketched, left_side=True, lower=True)  19.9 us
  transfers between devices with their start and end apart: 2, of which 2 were waited for; matrix products, arithmetic and copies ran while one was open for 0% of the time, Pallas kernels for 0%

commit v1 on v0

v1 whole, which is shorter than its diff:
```python
import jax
import jax.numpy as jnp
from jax import lax
from jax.experimental import pallas as pl
from jax.experimental.pallas import tpu as pltpu
from jax.sharding import PartitionSpec as P

highest = lax.Precision.HIGHEST
AXES = ("pts", "hrs")
BLOCK = 64


def dot_nn(left, right):
    return jnp.dot(left, right, precision=highest, preferred_element_type=jnp.float32)


def dot_tn(left, right):
    return lax.dot_general(
        left, right, (((0,), (0,)), ((), ())), precision=highest, preferred_element_type=jnp.float32
    )


def dot_nt(left, right):
    return lax.dot_general(
        left, right, (((1,), (1,)), ((), ())), precision=highest, preferred_element_type=jnp.float32
    )


def sketch_body(scale, fields_ref, probes_ref, sketched_ref, moment_ref):
    step = pl.program_id(0)
    devs, per, pts = fields_ref.shape
    hours = devs * per
    panel = fields_ref[...].reshape(hours, pts)
    sketched = dot_nn(probes_ref[...], panel)
    sketched_ref[...] = sketched
    moment = (dot_nt(sketched, panel) * scale).reshape(-1, 8, hours)

    @pl.when(step == 0)
    def _():
        for c in range(hours // 128):
            moment_ref[:, c] = moment[:, :, 128 * c : 128 * c + 128]

    @pl.when(step > 0)
    def _():
        for c in range(hours // 128):
            moment_ref[:, c] += moment[:, :, 128 * c : 128 * c + 128]


def sketch(panels, probes, scale, width=1024):
    devs, per, pts = panels.shape
    k, hours = probes.shape
    width = min(width, pts)
    return pl.pallas_call(
        lambda *refs: sketch_body(scale, *refs),
        name="sketch",
        grid=(pts // width,),
        in_specs=[
            pl.BlockSpec((devs, per, width), lambda i: (0, 0, i)),
            pl.BlockSpec((k, hours), lambda i: (0, 0)),
        ],
        out_specs=[
            pl.BlockSpec((k, width), lambda i: (0, i)),
            pl.BlockSpec((k // 8, hours // 128, 8, 128), lambda i: (0, 0, 0, 0)),
        ],
        out_shape=[
            jax.ShapeDtypeStruct((k, pts), jnp.float32),
            jax.ShapeDtypeStruct((k // 8, hours // 128, 8, 128), jnp.float32),
        ],
        compiler_params=pltpu.CompilerParams(vmem_limit_bytes=48 << 20),
    )(panels, probes)


def inverse_factor(block, left):
    n, lanes = block.shape
    row = lax.broadcasted_iota(jnp.int32, (n, lanes), 0)
    lane = lax.broadcasted_iota(jnp.int32, (n, lanes), 1)
    off = 0 if left else n
    for j in range(n):
        pivot = block[j : j + 1, off + j : off + j + 1]
        column = jnp.broadcast_to(block[:, off + j : off + j + 1], (n, lanes))
        block = block - jnp.where(row > j, column, 0.0) * (block[j : j + 1, :] * (1.0 / pivot))
    pivots = jnp.sum(jnp.where(lane == row + off, block, 0.0), axis=1, keepdims=True)
    block = block * lax.rsqrt(pivots)
    return block[:, n:] if left else block[:, :n]


def factor_body(moment_ref, probes_ref, sketched_ref, basis_ref, coeffs_ref, work_ref):
    tiles = moment_ref.shape[1]
    k = sketched_ref.shape[0]
    moment = jnp.concatenate([moment_ref[:, c].reshape(k, 128) for c in range(tiles)], axis=1)
    row = lax.broadcasted_iota(jnp.int32, (k, k), 0)
    col = lax.broadcasted_iota(jnp.int32, (k, k), 1)
    work_ref[:, :k] = dot_nt(moment, probes_ref[...])
    work_ref[:, k:] = jnp.where(row == col, 1.0, 0.0)
    n = BLOCK
    brow = lax.broadcasted_iota(jnp.int32, (n, 2 * n), 0)
    blane = lax.broadcasted_iota(jnp.int32, (n, 2 * n), 1)
    for b in range(k // n):
        lo = n * b
        left = b % 2 == 0
        lane0 = 2 * n * (b // 2)
        block = work_ref[lo : lo + n, lane0 : lane0 + 2 * n]
        if left:
            block = jnp.where(blane < n, block, jnp.where(blane - n == brow, 1.0, 0.0))
        else:
            block = jnp.where(blane >= n, block, jnp.where(blane == brow, 1.0, 0.0))
        upper = dot_nn(inverse_factor(block, left), work_ref[lo : lo + n, :])
        work_ref[lo : lo + n, k:] = upper[:, k:]
        if lo + n < k:
            update = dot_tn(upper[:, :k], upper)
            work_ref[lo + n :, :] = work_ref[lo + n :, :] - update[lo + n :, :]
    inverse = work_ref[:, k:]
    basis_ref[...] = dot_nn(inverse, sketched_ref[...])
    coeffs_ref[...] = dot_nn(inverse, moment)


def factor_and_apply(moment, probes, sketched):
    k, pts = sketched.shape
    return pl.pallas_call(
        factor_body,
        name="factor_and_apply",
        out_shape=[
            jax.ShapeDtypeStruct((k, pts), jnp.float32),
            jax.ShapeDtypeStruct(probes.shape, jnp.float32),
        ],
        scratch_shapes=[pltpu.VMEM((k, 2 * k), jnp.float32)],
        compiler_params=pltpu.CompilerParams(vmem_limit_bytes=48 << 20),
    )(moment, probes, sketched)


def on_device(fields, probes):
    devices = lax.axis_size("pts") * lax.axis_size("hrs")
    per, n_points = fields.shape
    sent = fields.reshape(per, devices, n_points // devices).transpose(1, 0, 2)
    panels = lax.all_to_all(sent, AXES, split_axis=0, concat_axis=0, tiled=True)
    sketched, moment = sketch(panels, probes, 1.0 / n_points)
    parts = moment.reshape(devices, -1, 128)
    parts = lax.all_to_all(parts, AXES, split_axis=0, concat_axis=0, tiled=True)
    total = jnp.broadcast_to(jnp.sum(parts, axis=0)[None], parts.shape)
    total = lax.all_to_all(total, AXES, split_axis=0, concat_axis=0, tiled=True)
    basis_rows, coeffs = factor_and_apply(total.reshape(moment.shape), probes, sketched)
    return (basis_rows, coeffs)


def solution(mesh):
    return jax.shard_map(
        on_device,
        mesh=mesh,
        in_specs=(P(AXES, None), P()),
        out_specs=(P(None, AXES), P()),
        check_vma=False,
    )
```

time: 446 us -> 139 us (0.31)
  waiting for transfers between devices: 280 us -> 0 us
  other arithmetic: 54.8 us -> 0.14 us
  Pallas kernels: 0 us -> 37.5 us
  blocking collectives: 64.6 us -> 100 us
  matrix products: 16.1 us -> 0 us
  between operations: 15.4 us -> 0.65 us
  local copies, waits for them, and re-layouts: 14.3 us -> 0.04 us
    psum x2 -> x0, waiting for transfers between devices: 280 us -> none  [the longest x1 143 us: on_device(): lax.psum(contract_last(basis_rows, panels) / n_points, ('pts', 'hrs'))]
    another operation x10 -> x0, other arithmetic: 53.8 us -> none  [the longest x6 34 us: on_device(): factor = jnp.linalg.cholesky(gram_sum)]
    pallas_call x0 -> x2, Pallas kernels: none -> 37.5 us  [the longest x1 28.4 us: factor_and_apply(): pl.pallas_call(factor_body, name='factor_and_apply', out_shape=[jax.Shape...]
    all_to_all x1 -> x3, blocking collectives: 64.6 us -> 100 us  [the longest x1 64.6 us: on_device(): panels = lax.all_to_all(sent, AXES, split_axis=0, concat_axis=0, tiled=True)]
    dot_general x3 -> x0, matrix products: 12.5 us -> none  [the longest x2 7.08 us: contract_last(): lax.dot_general(left, right, (((1,), (1,)), ((), ())), precision=highest,...]
    all_to_all x1 -> x0, local copies, waits for them, and re-layouts: 5.28 us -> none  [on_device(): lax.all_to_all(fields, ('pts', 'hrs'), split_axis=1, concat_axis=0, tiled...]
  transfers between devices with their start and end apart: 2 -> 0, of which waited for: 2 -> 0; matrix products, arithmetic and copies ran while one was open for 0% -> 0% of each run, Pallas kernels for 0% -> 0%
where the time goes in v1:
time: 139 us
  blocking collectives  100 us (72%)
  Pallas kernels  37.5 us (27%)
    all_to_all x1, blocking collectives, on_device(): panels = lax.all_to_all(sent, AXES, split_axis=0, concat_axis=0, tiled=True)  64.6 us
    pallas_call x1, Pallas kernels, factor_and_apply(): pl.pallas_call(factor_body, name='factor_and_apply', out_shape=[jax.Shape...  28.4 us
    all_to_all x1, blocking collectives, on_device(): total = lax.all_to_all(total, AXES, split_axis=0, concat_axis=0, tiled=True)  18 us
    all_to_all x1, blocking collectives, on_device(): parts = lax.all_to_all(parts, AXES, split_axis=0, concat_axis=0, tiled=True)  17.6 us
    pallas_call x1, Pallas kernels, sketch(): pl.pallas_call(lambda *refs: sketch_body(scale, *refs), name='sketch', gr...  9.04 us

profile of v1, /device:TPU:1, one launch (start us, length us, event | category | flops | bytes accessed | tf_op | source)
XLA Modules:
  0.0 138.5 jit_solution(11544778224247653552)
XLA Ops:
  0.6 0.0 copy-start
  0.6 64.6 %all_to_all.15.refs_0_ = f32[128,4,2048]{2,1,0:T(4,128)} all-to-all(f32[128,4,2048]{2,1,0:T(4,128)} %bitcast.7), channel_id=1, replica_groups=mesh['pts'=16,'hrs'=8] {'pts','hrs'}, dimensions={0} | all-to-all | bytes 8388608 | tf_op jit(solution)/shard_map/all_to_all | solution.py:135
  65.3 0.0 copy-done
  65.3 9.0 %sketch.1 = (f32[256,2048]{1,0:T(8,128)S(1)}, f32[32,4,8,128]{3,2,1,0:T(8,128)S(1)}) custom-call(f32[128,4,2048]{2,1,0:T(4,128)} %all_to_all.15.refs_0_, f32[256,512]{1,0:T(8,128)S(1)} %copy-done), custom_call_target="tpu_custom_call" | custom-call | tf_op jit(solution)/shard_map/sketch/pallas_call | solution.py:53
  74.3 17.6 %all_to_all.16 = f32[128,8,128]{2,1,0:T(8,128)S(1)} all-to-all(f32[128,8,128]{2,1,0:T(8,128)S(1)} %bitcast.6), channel_id=1, replica_groups=mesh['pts'=16,'hrs'=8] {'pts','hrs'}, dimensions={0} | all-to-all | bytes 1048576 | tf_op jit(solution)/shard_map/all_to_all | solution.py:138
  91.9 0.1 reduce_sum.9
  92.1 18.0 %all_to_all.17 = f32[128,8,128]{2,1,0:T(8,128)S(1)} all-to-all(f32[128,8,128]{2,1,0:T(8,128)S(1)} %broadcast_in_dim.2), channel_id=1, replica_groups=mesh['pts'=16,'hrs'=8] {'pts','hrs'}, dimensions={0} | all-to-all | bytes 1048576 | tf_op jit(solution)/shard_map/all_to_all | solution.py:140
  110.1 28.4 %factor_and_apply.1 = (f32[256,2048]{1,0:T(8,128)}, f32[256,512]{1,0:T(8,128)}) custom-call(f32[32,4,8,128]{3,2,1,0:T(8,128)S(1)} %bitcast.5, f32[256,512]{1,0:T(8,128)S(1)} %copy-done, f32[256,2048]{1,0:T(8,128)S(1)} %get-tuple-element.5.sketched_ref), custom_call_target="tpu_custom_call" | custom-call | tf_op jit(solution)/shard_map/factor_and_apply/pallas_call | solution.py:119
  (1 shorter events, 0.0 us)
Async XLA Ops:
  0.6 64.6 %copy-start = (f32[256,512]{1,0:T(8,128)S(1)}, f32[256,512]{1,0:T(8,128)}, u32[]{:S(2)}) copy-start(f32[256,512]{1,0:T(8,128)} %probes_ref.1) | copy-start | bytes 1572868

commit v2 on v1

--- a/solution.py
+++ b/solution.py
@@ -70,17 +70,42 @@
     )(panels, probes)
 
 
+def spread(x):
+    return jnp.broadcast_to(x, (8, 128))
+
+
 def inverse_factor(block, left):
-    n, lanes = block.shape
-    row = lax.broadcasted_iota(jnp.int32, (n, lanes), 0)
-    lane = lax.broadcasted_iota(jnp.int32, (n, lanes), 1)
+    n = block.shape[0]
     off = 0 if left else n
-    for j in range(n):
-        pivot = block[j : j + 1, off + j : off + j + 1]
-        column = jnp.broadcast_to(block[:, off + j : off + j + 1], (n, lanes))
-        block = block - jnp.where(row > j, column, 0.0) * (block[j : j + 1, :] * (1.0 / pivot))
-    pivots = jnp.sum(jnp.where(lane == row + off, block, 0.0), axis=1, keepdims=True)
-    block = block * lax.rsqrt(pivots)
+    sublane = lax.broadcasted_iota(jnp.int32, (8, 128), 0)
+    tiles = [block[8 * v : 8 * v + 8, :] for v in range(n // 8)]
+    done = []
+    for t in range(n // 8):
+        cols = {}
+        for v in range(t, n // 8):
+            for i in range(8):
+                lane = off + 8 * t + i
+                cols[v, i] = spread(tiles[v][:, lane : lane + 1])
+        rows = [spread(tiles[t][i : i + 1, :]) for i in range(8)]
+        inverses = []
+        pivots = None
+        for i in range(8):
+            pivot = spread(cols[t, i][i : i + 1, :])
+            pivots = pivot if i == 0 else jnp.where(sublane == i, pivot, pivots)
+            inverses.append(1.0 / pivot)
+            for j in range(i + 1, 8):
+                ratio = inverses[i] * spread(cols[t, j][i : i + 1, :])
+                for v in range(t, n // 8):
+                    cols[v, j] = cols[v, j] - cols[v, i] * ratio
+                rows[j] = rows[j] - ratio * rows[i]
+        for v in range(t + 1, n // 8):
+            for i in range(8):
+                tiles[v] = tiles[v] - (cols[v, i] * inverses[i]) * rows[i]
+        tile = rows[0]
+        for i in range(1, 8):
+            tile = jnp.where(sublane == i, rows[i], tile)
+        done.append(tile * lax.rsqrt(pivots))
+    block = jnp.concatenate(done, axis=0)
     return block[:, n:] if left else block[:, :n]
 
 

time: 139 us -> 124 us (0.89)
  Pallas kernels: 37.5 us -> 23 us
    pallas_call x1, Pallas kernels: 28.4 us -> 13.9 us  [factor_and_apply(): pl.pallas_call(factor_body, name='factor_and_apply', out_shape=[jax.Shape...]
where the time goes in v2:
time: 124 us
  blocking collectives  100 us (81%)
  Pallas kernels  23 us (19%)
    all_to_all x1, blocking collectives, on_device(): panels = lax.all_to_all(sent, AXES, split_axis=0, concat_axis=0, tiled=True)  64.6 us
    all_to_all x1, blocking collectives, on_device(): total = lax.all_to_all(total, AXES, split_axis=0, concat_axis=0, tiled=True)  18 us
    all_to_all x1, blocking collectives, on_device(): parts = lax.all_to_all(parts, AXES, split_axis=0, concat_axis=0, tiled=True)  17.6 us
    pallas_call x1, Pallas kernels, factor_and_apply(): pl.pallas_call(factor_body, name='factor_and_apply', out_shape=[jax.Shape...  13.9 us
    pallas_call x1, Pallas kernels, sketch(): pl.pallas_call(lambda *refs: sketch_body(scale, *refs), name='sketch', gr...  9.04 us

profile of v2, /device:TPU:1, one launch (start us, length us, event | category | flops | bytes accessed | tf_op | source)
XLA Modules:
  0.0 124.0 jit_solution(9264046008316318584)
XLA Ops:
  0.6 0.0 copy-start
  0.6 64.6 %all_to_all.15.refs_0_ = f32[128,4,2048]{2,1,0:T(4,128)} all-to-all(f32[128,4,2048]{2,1,0:T(4,128)} %bitcast.7), channel_id=1, replica_groups=mesh['pts'=16,'hrs'=8] {'pts','hrs'}, dimensions={0} | all-to-all | bytes 8388608 | tf_op jit(solution)/shard_map/all_to_all | solution.py:160
  65.3 0.0 copy-done
  65.3 9.0 %sketch.1 = (f32[256,2048]{1,0:T(8,128)S(1)}, f32[32,4,8,128]{3,2,1,0:T(8,128)S(1)}) custom-call(f32[128,4,2048]{2,1,0:T(4,128)} %all_to_all.15.refs_0_, f32[256,512]{1,0:T(8,128)S(1)} %copy-done), custom_call_target="tpu_custom_call" | custom-call | tf_op jit(solution)/shard_map/sketch/pallas_call | solution.py:53
  74.3 17.6 %all_to_all.16 = f32[128,8,128]{2,1,0:T(8,128)S(1)} all-to-all(f32[128,8,128]{2,1,0:T(8,128)S(1)} %bitcast.6), channel_id=1, replica_groups=mesh['pts'=16,'hrs'=8] {'pts','hrs'}, dimensions={0} | all-to-all | bytes 1048576 | tf_op jit(solution)/shard_map/all_to_all | solution.py:163
  91.9 0.1 reduce_sum.9
  92.1 18.0 %all_to_all.17 = f32[128,8,128]{2,1,0:T(8,128)S(1)} all-to-all(f32[128,8,128]{2,1,0:T(8,128)S(1)} %broadcast_in_dim.2), channel_id=1, replica_groups=mesh['pts'=16,'hrs'=8] {'pts','hrs'}, dimensions={0} | all-to-all | bytes 1048576 | tf_op jit(solution)/shard_map/all_to_all | solution.py:165
  110.1 13.9 %factor_and_apply.1 = (f32[256,2048]{1,0:T(8,128)}, f32[256,512]{1,0:T(8,128)}) custom-call(f32[32,4,8,128]{3,2,1,0:T(8,128)S(1)} %bitcast.5, f32[256,512]{1,0:T(8,128)S(1)} %copy-done, f32[256,2048]{1,0:T(8,128)S(1)} %get-tuple-element.5.sketched_ref), custom_call_target="tpu_custom_call" | custom-call | tf_op jit(solution)/shard_map/factor_and_apply/pallas_call | solution.py:144
  (1 shorter events, 0.0 us)
Async XLA Ops:
  0.6 64.6 %copy-start = (f32[256,512]{1,0:T(8,128)S(1)}, f32[256,512]{1,0:T(8,128)}, u32[]{:S(2)}) copy-start(f32[256,512]{1,0:T(8,128)} %probes_ref.1) | copy-start | bytes 1572868

commit v3 on v0

v3 whole, which is shorter than its diff:
```python
import jax
import jax.numpy as jnp
from jax import lax
from jax.experimental import pallas as pl
from jax.experimental.pallas import tpu as pltpu
from jax.sharding import PartitionSpec as P

highest = lax.Precision.HIGHEST
AXES = ("pts", "hrs")
CHUNK = 512
HALF = 128
BLOCK = 32
PANEL = 16


def dot_nn(left, right):
    return jnp.dot(left, right, precision=highest, preferred_element_type=jnp.float32)


def dot_tn(left, right):
    return lax.dot_general(
        left, right, (((0,), (0,)), ((), ())), precision=highest, preferred_element_type=jnp.float32
    )


def dot_nt(left, right):
    return lax.dot_general(
        left, right, (((1,), (1,)), ((), ())), precision=highest, preferred_element_type=jnp.float32
    )


def split(x):
    high = x.astype(jnp.bfloat16)
    return high, (x - high.astype(jnp.float32)).astype(jnp.bfloat16)


def dot_split(left, right_high, right_low):
    high, low = split(left)
    return jnp.dot(
        jnp.concatenate([high, high, low], axis=1),
        jnp.concatenate([right_high, right_low, right_high], axis=0),
        preferred_element_type=jnp.float32,
    )


def sketch_body(scale, panels_ref, probes_ref, high_ref, low_ref, moment_ref, raw_ref, fields_high, fields_low, sems):
    count, devs, per, width = raw_ref.shape
    hours = devs * per
    copies = [
        pltpu.make_async_copy(panels_ref.at[:, :, width * c : width * c + width], raw_ref.at[c], sems.at[c])
        for c in range(count)
    ]
    for copy in copies:
        copy.start()
    probes = probes_ref[...]
    for c in range(count):
        copies[c].wait()
        cols = slice(width * c, width * c + width)
        high, low = split(raw_ref[c].reshape(hours, width))
        fields_high[:, cols] = high
        fields_low[:, cols] = low
        high_ref[:, cols], low_ref[:, cols] = split(dot_split(probes, high, low))
    high, low = high_ref[...], low_ref[...]
    moment = lax.dot_general(
        jnp.concatenate([high, high, low], axis=1),
        jnp.concatenate([fields_high[...], fields_low[...], fields_high[...]], axis=1),
        (((1,), (1,)), ((), ())),
        preferred_element_type=jnp.float32,
    )
    moment = (moment * scale).reshape(-1, 8, hours)
    for c in range(hours // 128):
        moment_ref[:, c] = moment[:, :, 128 * c : 128 * c + 128]


def sketch(panels, probes, scale):
    devs, per, pts = panels.shape
    k, hours = probes.shape
    width = min(CHUNK, pts)
    count = pts // width
    vmem = pl.BlockSpec(memory_space=pltpu.VMEM)
    return pl.pallas_call(
        lambda *refs: sketch_body(scale, *refs),
        name="sketch",
        in_specs=[pl.BlockSpec(memory_space=pl.ANY), vmem],
        out_specs=[vmem, vmem, vmem],
        out_shape=[
            jax.ShapeDtypeStruct((k, pts), jnp.bfloat16),
            jax.ShapeDtypeStruct((k, pts), jnp.bfloat16),
            jax.ShapeDtypeStruct((k // 8, hours // 128, 8, 128), jnp.float32),
        ],
        scratch_shapes=[
            pltpu.VMEM((count, devs, per, width), jnp.float32),
            pltpu.VMEM((hours, pts), jnp.bfloat16),
            pltpu.VMEM((hours, pts), jnp.bfloat16),
            pltpu.SemaphoreType.DMA((count,)),
        ],
        compiler_params=pltpu.CompilerParams(vmem_limit_bytes=48 << 20),
    )(panels, probes)


def spread(x):
    return jnp.broadcast_to(x, (8, 128))


def eliminate(tiles, offset):
    sublane = lax.broadcasted_iota(jnp.int32, (8, 128), 0)
    lane = lax.broadcasted_iota(jnp.int32, (8, 128), 1)
    tiles = list(tiles)
    count = len(tiles)
    done = []
    for t in range(0, count, PANEL // 8):
        first = offset + 8 * t
        own = (lane >= first) & (lane < first + PANEL)
        cols = {}
        for v in range(t, count):
            for i in range(PANEL):
                cols[v, i] = spread(tiles[v][:, first + i : first + i + 1])
        rows = []
        for u in range(PANEL // 8):
            unit = jnp.where(lane - first - 8 * u == sublane, 1.0, 0.0)
            tile = jnp.where(own, unit, tiles[t + u])
            rows += [spread(tile[i : i + 1, :]) for i in range(8)]
        inverses = []
        pivots = []
        for i in range(PANEL):
            v0, s = t + i // 8, i % 8
            pivots.append(spread(cols[v0, i][s : s + 1, :]))
            inverses.append(1.0 / pivots[i])
            for j in range(i + 1, PANEL):
                ratio = inverses[i] * spread(cols[v0, j][s : s + 1, :])
                for v in range(v0, count):
                    cols[v, j] = cols[v, j] - cols[v, i] * ratio
                rows[j] = rows[j] - ratio * rows[i]
        for v in range(t + PANEL // 8, count):
            tiles[v] = jnp.where(own, 0.0, tiles[v])
            for i in range(PANEL):
                tiles[v] = tiles[v] - (cols[v, i] * inverses[i]) * rows[i]
        for u in range(PANEL // 8):
            tile, pivot = rows[8 * u], pivots[8 * u]
            for i in range(1, 8):
                tile = jnp.where(sublane == i, rows[8 * u + i], tile)
                pivot = jnp.where(sublane == i, pivots[8 * u + i], pivot)
            done.append(tile * lax.rsqrt(pivot))
    return done


def inverse_factor(matrix):
    n = matrix.shape[0]
    row = lax.broadcasted_iota(jnp.int32, (n, n), 0)
    lane = lax.broadcasted_iota(jnp.int32, (n, n), 1)
    tiles = [matrix[8 * v : 8 * v + 8] for v in range(n // 8)]
    per = BLOCK // 8
    for b in range(n // BLOCK):
        lo = BLOCK * b
        here = slice(per * b, per * b + per)
        tiles[here] = eliminate(tiles[here], lo)
        if lo + BLOCK < n:
            block = jnp.concatenate(tiles[here], axis=0)
            above = (lane[:BLOCK] > row[:BLOCK] + lo) & (lane[:BLOCK] < lo + BLOCK)
            update = dot_tn(block, jnp.where(above, 0.0, block))
            own = (lane[:8] >= lo) & (lane[:8] < lo + BLOCK)
            for v in range(per * b + per, n // 8):
                tiles[v] = jnp.where(own, 0.0, tiles[v]) - update[8 * v : 8 * v + 8]
    return jnp.where(lane <= row, jnp.concatenate(tiles, axis=0), 0.0)


def factor_body(moment_ref, probes_ref, high_ref, low_ref, basis_ref, coeffs_ref, out_ref, sems):
    n = HALF
    k = high_ref.shape[0]
    moment = jnp.concatenate([moment_ref[:, c].reshape(k, 128) for c in range(moment_ref.shape[1])], axis=1)
    probes = probes_ref[...]
    moment_high, moment_low = split(moment)

    def apply(part, inverse):
        rows = pl.ds(part * n, n)
        used = inverse.shape[1]
        out_ref[rows, :] = dot_split(inverse, high_ref[:used, :], low_ref[:used, :])
        copy = pltpu.make_async_copy(out_ref.at[rows, :], basis_ref.at[rows, :], sems.at[part])
        copy.start()
        coeffs_ref[rows, :] = dot_split(inverse, moment_high[:used], moment_low[:used])
        return copy

    upper = inverse_factor(dot_nt(moment[:n], probes[:n]))
    cross = dot_nn(upper, dot_nt(moment[:n], probes[n:]))
    lower = inverse_factor(dot_nt(moment[n:], probes[n:]) - dot_tn(cross, cross))
    first = apply(0, upper)
    corner = dot_nn(lower, dot_tn(cross, upper))
    second = apply(1, jnp.concatenate([-corner, lower], axis=1))
    first.wait()
    second.wait()


def factor_and_apply(moment, probes, high, low):
    k, pts = high.shape
    vmem = pl.BlockSpec(memory_space=pltpu.VMEM)
    return pl.pallas_call(
        factor_body,
        name="factor_and_apply",
        in_specs=[vmem, vmem, vmem, vmem],
        out_specs=[pl.BlockSpec(memory_space=pl.ANY), vmem],
        out_shape=[
            jax.ShapeDtypeStruct((k, pts), jnp.float32),
            jax.ShapeDtypeStruct(probes.shape, jnp.float32),
        ],
        scratch_shapes=[pltpu.VMEM((k, pts), jnp.float32), pltpu.SemaphoreType.DMA((2,))],
        compiler_params=pltpu.CompilerParams(vmem_limit_bytes=48 << 20),
    )(moment, probes, high, low)


def on_device(fields, probes):
    devices = lax.axis_size("pts") * lax.axis_size("hrs")
    per, n_points = fields.shape
    sent = fields.reshape(per, devices, n_points // devices).transpose(1, 0, 2)
    panels = lax.all_to_all(sent, AXES, split_axis=0, concat_axis=0, tiled=True)
    high, low, moment = sketch(panels, probes, 1.0 / n_points)
    parts = moment.reshape(devices, -1, 128)
    parts = lax.all_to_all(parts, AXES, split_axis=0, concat_axis=0, tiled=True)
    total = jnp.broadcast_to(jnp.sum(parts, axis=0)[None], parts.shape)
    total = lax.all_to_all(total, AXES, split_axis=0, concat_axis=0, tiled=True)
    basis_rows, coeffs = factor_and_apply(total.reshape(moment.shape), probes, high, low)
    return (basis_rows, coeffs)


def solution(mesh):
    return jax.shard_map(
        on_device,
        mesh=mesh,
        in_specs=(P(AXES, None), P()),
        out_specs=(P(None, AXES), P()),
        check_vma=False,
    )
```

time: 446 us -> 117 us (0.26)
  waiting for transfers between devices: 280 us -> 0 us
  other arithmetic: 54.8 us -> 0.14 us
  blocking collectives: 64.6 us -> 100 us
  matrix products: 16.1 us -> 0 us
  Pallas kernels: 0 us -> 15.8 us
  between operations: 15.4 us -> 0.81 us
  local copies, waits for them, and re-layouts: 14.3 us -> 0.04 us
    psum x2 -> x0, waiting for transfers between devices: 280 us -> none  [the longest x1 143 us: on_device(): lax.psum(contract_last(basis_rows, panels) / n_points, ('pts', 'hrs'))]
    another operation x10 -> x0, other arithmetic: 53.8 us -> none  [the longest x6 34 us: on_device(): factor = jnp.linalg.cholesky(gram_sum)]
    all_to_all x1 -> x3, blocking collectives: 64.6 us -> 100 us  [the longest x1 64.6 us: on_device(): panels = lax.all_to_all(sent, AXES, split_axis=0, concat_axis=0, tiled=True)]
    pallas_call x0 -> x2, Pallas kernels: none -> 15.8 us  [the longest x1 10.6 us: factor_and_apply(): pl.pallas_call(factor_body, name='factor_and_apply', in_specs=[vmem, vmem...]
    dot_general x3 -> x0, matrix products: 12.5 us -> none  [the longest x2 7.08 us: contract_last(): lax.dot_general(left, right, (((1,), (1,)), ((), ())), precision=highest,...]
    all_to_all x1 -> x0, local copies, waits for them, and re-layouts: 5.28 us -> none  [on_device(): lax.all_to_all(fields, ('pts', 'hrs'), split_axis=1, concat_axis=0, tiled...]
  transfers between devices with their start and end apart: 2 -> 0, of which waited for: 2 -> 0; matrix products, arithmetic and copies ran while one was open for 0% -> 0% of each run, Pallas kernels for 0% -> 0%
where the time goes in v3:
time: 117 us
  blocking collectives  100 us (85%)
  Pallas kernels  15.8 us (14%)
    all_to_all x1, blocking collectives, on_device(): panels = lax.all_to_all(sent, AXES, split_axis=0, concat_axis=0, tiled=True)  64.6 us
    all_to_all x1, blocking collectives, on_device(): total = lax.all_to_all(total, AXES, split_axis=0, concat_axis=0, tiled=True)  18 us
    all_to_all x1, blocking collectives, on_device(): parts = lax.all_to_all(parts, AXES, split_axis=0, concat_axis=0, tiled=True)  17.6 us
    pallas_call x1, Pallas kernels, factor_and_apply(): pl.pallas_call(factor_body, name='factor_and_apply', in_specs=[vmem, vmem...  10.6 us
    pallas_call x1, Pallas kernels, sketch(): pl.pallas_call(lambda *refs: sketch_body(scale, *refs), name='sketch', in...  5.29 us

profile of v3, /device:TPU:1, one launch (start us, length us, event | category | flops | bytes accessed | tf_op | source)
XLA Modules:
  0.0 117.1 jit_solution(3703071593095541431)
XLA Ops:
  0.6 0.0 copy-start
  0.6 64.6 %all_to_all.15.refs_0_ = f32[128,4,2048]{2,1,0:T(4,128)} all-to-all(f32[128,4,2048]{2,1,0:T(4,128)} %bitcast.7), channel_id=1, replica_groups=mesh['pts'=16,'hrs'=8] {'pts','hrs'}, dimensions={0} | all-to-all | bytes 8388608 | tf_op jit(solution)/shard_map/all_to_all | solution.py:214
  65.3 0.0 copy-done
  65.3 5.3 %sketch.1 = (bf16[256,2048]{1,0:T(8,128)(2,1)S(1)}, bf16[256,2048]{1,0:T(8,128)(2,1)S(1)}, f32[32,4,8,128]{3,2,1,0:T(8,128)S(1)}) custom-call(f32[128,4,2048]{2,1,0:T(4,128)} %all_to_all.15.refs_0_, f32[256,512]{1,0:T(8,128)S(1)} %copy-done), custom_call_target="tpu_custom_call" | custom-call | tf_op jit(solution)/shard_map/sketch/pallas_call | solution.py:81
  70.5 17.6 %all_to_all.16 = f32[128,8,128]{2,1,0:T(8,128)S(1)} all-to-all(f32[128,8,128]{2,1,0:T(8,128)S(1)} %bitcast.6), channel_id=1, replica_groups=mesh['pts'=16,'hrs'=8] {'pts','hrs'}, dimensions={0} | all-to-all | bytes 1048576 | tf_op jit(solution)/shard_map/all_to_all | solution.py:217
  88.1 0.1 reduce_sum.9
  88.3 18.0 %all_to_all.17 = f32[128,8,128]{2,1,0:T(8,128)S(1)} all-to-all(f32[128,8,128]{2,1,0:T(8,128)S(1)} %broadcast_in_dim.2), channel_id=1, replica_groups=mesh['pts'=16,'hrs'=8] {'pts','hrs'}, dimensions={0} | all-to-all | bytes 1048576 | tf_op jit(solution)/shard_map/all_to_all | solution.py:219
  106.3 10.6 %factor_and_apply.1 = (f32[256,2048]{1,0:T(8,128)}, f32[256,512]{1,0:T(8,128)}) custom-call(f32[32,4,8,128]{3,2,1,0:T(8,128)S(1)} %bitcast.5, f32[256,512]{1,0:T(8,128)S(1)} %copy-done, bf16[256,2048]{1,0:T(8,128)(2,1)S(1)} %get-tuple-element.6.high_ref, bf16[256,2048]{1,0:T(8,128)(2,1)S(1)} %get-tuple-element.7.low_ref), custom_call_target="tpu_custom_call" | custom-call | tf_op jit(solution)/shard_map/factor_and_apply/pallas_call | solution.py:196
  (1 shorter events, 0.0 us)
Async XLA Ops:
  0.6 64.6 %copy-start = (f32[256,512]{1,0:T(8,128)S(1)}, f32[256,512]{1,0:T(8,128)}, u32[]{:S(2)}) copy-start(f32[256,512]{1,0:T(8,128)} %probes_ref.1) | copy-start | bytes 1572868

commit v4 on v3

--- a/solution.py
+++ b/solution.py
@@ -43,20 +43,14 @@
     )
 
 
-def sketch_body(scale, panels_ref, probes_ref, high_ref, low_ref, moment_ref, raw_ref, fields_high, fields_low, sems):
-    count, devs, per, width = raw_ref.shape
+def sketch_body(scale, panels_ref, probes_ref, high_ref, low_ref, moment_ref, fields_high, fields_low):
+    devs, per, pts = panels_ref.shape
     hours = devs * per
-    copies = [
-        pltpu.make_async_copy(panels_ref.at[:, :, width * c : width * c + width], raw_ref.at[c], sems.at[c])
-        for c in range(count)
-    ]
-    for copy in copies:
-        copy.start()
+    width = min(CHUNK, pts)
     probes = probes_ref[...]
-    for c in range(count):
-        copies[c].wait()
+    for c in range(pts // width):
         cols = slice(width * c, width * c + width)
-        high, low = split(raw_ref[c].reshape(hours, width))
+        high, low = split(panels_ref[:, :, cols].reshape(hours, width))
         fields_high[:, cols] = high
         fields_low[:, cols] = low
         high_ref[:, cols], low_ref[:, cols] = split(dot_split(probes, high, low))
@@ -75,13 +69,11 @@
 def sketch(panels, probes, scale):
     devs, per, pts = panels.shape
     k, hours = probes.shape
-    width = min(CHUNK, pts)
-    count = pts // width
     vmem = pl.BlockSpec(memory_space=pltpu.VMEM)
     return pl.pallas_call(
         lambda *refs: sketch_body(scale, *refs),
         name="sketch",
-        in_specs=[pl.BlockSpec(memory_space=pl.ANY), vmem],
+        in_specs=[vmem, vmem],
         out_specs=[vmem, vmem, vmem],
         out_shape=[
             jax.ShapeDtypeStruct((k, pts), jnp.bfloat16),
@@ -89,12 +81,10 @@
             jax.ShapeDtypeStruct((k // 8, hours // 128, 8, 128), jnp.float32),
         ],
         scratch_shapes=[
-            pltpu.VMEM((count, devs, per, width), jnp.float32),
             pltpu.VMEM((hours, pts), jnp.bfloat16),
             pltpu.VMEM((hours, pts), jnp.bfloat16),
-            pltpu.SemaphoreType.DMA((count,)),
         ],
-        compiler_params=pltpu.CompilerParams(vmem_limit_bytes=48 << 20),
+        compiler_params=pltpu.CompilerParams(vmem_limit_bytes=32 << 20),
     )(panels, probes)
 
 
@@ -107,41 +97,37 @@
     lane = lax.broadcasted_iota(jnp.int32, (8, 128), 1)
     tiles = list(tiles)
     count = len(tiles)
-    done = []
     for t in range(0, count, PANEL // 8):
         first = offset + 8 * t
         own = (lane >= first) & (lane < first + PANEL)
         cols = {}
+        for i in range(PANEL):
+            for v in range(t + i // 8, count):
+                cols[v, i] = spread(tiles[v][:, first + i : first + i + 1])
         for v in range(t, count):
-            for i in range(PANEL):
-                cols[v, i] = spread(tiles[v][:, first + i : first + i + 1])
-        rows = []
-        for u in range(PANEL // 8):
-            unit = jnp.where(lane - first - 8 * u == sublane, 1.0, 0.0)
-            tile = jnp.where(own, unit, tiles[t + u])
-            rows += [spread(tile[i : i + 1, :]) for i in range(8)]
-        inverses = []
-        pivots = []
+            tiles[v] = jnp.where(own, jnp.where(lane - first - 8 * (v - t) == sublane, 1.0, 0.0), tiles[v])
         for i in range(PANEL):
-            v0, s = t + i // 8, i % 8
-            pivots.append(spread(cols[v0, i][s : s + 1, :]))
-            inverses.append(1.0 / pivots[i])
+            top, s = t + i // 8, i % 8
+            pivot = spread(cols[top, i][s : s + 1, :])
+            pivots = pivot if s == 0 else jnp.where(sublane == s, pivot, pivots)
+            inverse = 1.0 / pivot
+            scaled = {v: cols[v, i] * inverse for v in range(top, count)}
             for j in range(i + 1, PANEL):
-                ratio = inverses[i] * spread(cols[v0, j][s : s + 1, :])
-                for v in range(v0, count):
+                u, r = t + j // 8, j % 8
+                if j == i + 1:
+                    ratio = inverse * spread(cols[u, i][r : r + 1, :])
+                else:
+                    ratio = spread(scaled[u][r : r + 1, :])
+                for v in range(u, count):
                     cols[v, j] = cols[v, j] - cols[v, i] * ratio
-                rows[j] = rows[j] - ratio * rows[i]
-        for v in range(t + PANEL // 8, count):
-            tiles[v] = jnp.where(own, 0.0, tiles[v])
-            for i in range(PANEL):
-                tiles[v] = tiles[v] - (cols[v, i] * inverses[i]) * rows[i]
-        for u in range(PANEL // 8):
-            tile, pivot = rows[8 * u], pivots[8 * u]
-            for i in range(1, 8):
-                tile = jnp.where(sublane == i, rows[8 * u + i], tile)
-                pivot = jnp.where(sublane == i, pivots[8 * u + i], pivot)
-            done.append(tile * lax.rsqrt(pivot))
-    return done
+            row = spread(tiles[top][s : s + 1, :])
+            if s < 7:
+                tiles[top] = tiles[top] - jnp.where(sublane > s, scaled[top], 0.0) * row
+            for v in range(top + 1, count):
+                tiles[v] = tiles[v] - scaled[v] * row
+            if s == 7:
+                tiles[top] = tiles[top] * lax.rsqrt(pivots)
+    return tiles
 
 
 def inverse_factor(matrix):
@@ -166,28 +152,34 @@
 
 def factor_body(moment_ref, probes_ref, high_ref, low_ref, basis_ref, coeffs_ref, out_ref, sems):
     n = HALF
-    k = high_ref.shape[0]
+    k, pts = high_ref.shape
     moment = jnp.concatenate([moment_ref[:, c].reshape(k, 128) for c in range(moment_ref.shape[1])], axis=1)
     probes = probes_ref[...]
-    moment_high, moment_low = split(moment)
-
-    def apply(part, inverse):
-        rows = pl.ds(part * n, n)
-        used = inverse.shape[1]
-        out_ref[rows, :] = dot_split(inverse, high_ref[:used, :], low_ref[:used, :])
-        copy = pltpu.make_async_copy(out_ref.at[rows, :], basis_ref.at[rows, :], sems.at[part])
-        copy.start()
-        coeffs_ref[rows, :] = dot_split(inverse, moment_high[:used], moment_low[:used])
-        return copy
+    copies = []
+
+    def write(rows, cols, values):
+        where = (pl.ds(rows, values.shape[0]), pl.ds(cols, values.shape[1]))
+        out_ref[where] = values
+        copies.append(pltpu.make_async_copy(out_ref.at[where], basis_ref.at[where], sems.at[len(copies)]))
+        copies[-1].start()
 
     upper = inverse_factor(dot_nt(moment[:n], probes[:n]))
     cross = dot_nn(upper, dot_nt(moment[:n], probes[n:]))
-    lower = inverse_factor(dot_nt(moment[n:], probes[n:]) - dot_tn(cross, cross))
-    first = apply(0, upper)
-    corner = dot_nn(lower, dot_tn(cross, upper))
-    second = apply(1, jnp.concatenate([-corner, lower], axis=1))
-    first.wait()
-    second.wait()
+    rest = dot_nt(moment[n:], probes[n:]) - dot_tn(cross, cross)
+    basis = dot_split(upper, high_ref[:n, :], low_ref[:n, :])
+    write(0, 0, basis)
+    coeffs = dot_split(upper, *split(moment[:n]))
+    coeffs_ref[:n, :] = coeffs
+    second = high_ref[n:, :].astype(jnp.float32) + low_ref[n:, :].astype(jnp.float32)
+    high, low = split(second - dot_split(cross.T, *split(basis)))
+    moment_high, moment_low = split(moment[n:] - dot_split(cross.T, *split(coeffs)))
+    lower = inverse_factor(rest)
+    coeffs_ref[n:, :] = dot_split(lower, moment_high, moment_low)
+    for c in range(0, pts, pts // 2):
+        cols = slice(c, c + pts // 2)
+        write(n, c, dot_split(lower, high[:, cols], low[:, cols]))
+    for copy in copies:
+        copy.wait()
 
 
 def factor_and_apply(moment, probes, high, low):
@@ -202,8 +194,8 @@
             jax.ShapeDtypeStruct((k, pts), jnp.float32),
             jax.ShapeDtypeStruct(probes.shape, jnp.float32),
         ],
-        scratch_shapes=[pltpu.VMEM((k, pts), jnp.float32), pltpu.SemaphoreType.DMA((2,))],
-        compiler_params=pltpu.CompilerParams(vmem_limit_bytes=48 << 20),
+        scratch_shapes=[pltpu.VMEM((k, pts), jnp.float32), pltpu.SemaphoreType.DMA((3,))],
+        compiler_params=pltpu.CompilerParams(vmem_limit_bytes=32 << 20),
     )(moment, probes, high, low)
 
 

time: 117 us -> 114 us (0.974)
  Pallas kernels: 15.8 us -> 13.3 us
    pallas_call x1, Pallas kernels: 5.29 us -> 3.6 us  [sketch(): pl.pallas_call(lambda *refs: sketch_body(scale, *refs), name='sketch', in...]
where the time goes in v4:
time: 114 us
  blocking collectives  100 us (88%)
  Pallas kernels  13.3 us (12%)
    all_to_all x1, blocking collectives, on_device(): panels = lax.all_to_all(sent, AXES, split_axis=0, concat_axis=0, tiled=True)  64.5 us
    all_to_all x1, blocking collectives, on_device(): total = lax.all_to_all(total, AXES, split_axis=0, concat_axis=0, tiled=True)  18 us
    all_to_all x1, blocking collectives, on_device(): parts = lax.all_to_all(parts, AXES, split_axis=0, concat_axis=0, tiled=True)  17.6 us
    pallas_call x1, Pallas kernels, factor_and_apply(): pl.pallas_call(factor_body, name='factor_and_apply', in_specs=[vmem, vmem...  9.67 us
    pallas_call x1, Pallas kernels, sketch(): pl.pallas_call(lambda *refs: sketch_body(scale, *refs), name='sketch', in...  3.6 us

profile of v4, /device:TPU:1, one launch (start us, length us, event | category | flops | bytes accessed | tf_op | source)
XLA Modules:
  0.0 114.2 jit_solution(3200558634713845765)
XLA Ops:
  0.6 0.0 copy-start
  0.6 64.5 %all_to_all.15.refs_0_ = f32[128,4,2048]{2,1,0:T(4,128)S(1)} all-to-all(f32[128,4,2048]{2,1,0:T(4,128)} %bitcast.7), channel_id=1, replica_groups=mesh['pts'=16,'hrs'=8] {'pts','hrs'}, dimensions={0} | all-to-all | bytes 8388608 | tf_op jit(solution)/shard_map/all_to_all | solution.py:206
  65.1 0.0 copy-done
  65.1 3.6 %sketch.1 = (bf16[256,2048]{1,0:T(8,128)(2,1)S(1)}, bf16[256,2048]{1,0:T(8,128)(2,1)S(1)}, f32[32,4,8,128]{3,2,1,0:T(8,128)S(1)}) custom-call(f32[128,4,2048]{2,1,0:T(4,128)S(1)} %all_to_all.15.refs_0_, f32[256,512]{1,0:T(8,128)S(1)} %copy-done), custom_call_target="tpu_custom_call" | custom-call | tf_op jit(solution)/shard_map/sketch/pallas_call | solution.py:73
  68.8 17.6 %all_to_all.16 = f32[128,8,128]{2,1,0:T(8,128)S(1)} all-to-all(f32[128,8,128]{2,1,0:T(8,128)S(1)} %bitcast.6), channel_id=1, replica_groups=mesh['pts'=16,'hrs'=8] {'pts','hrs'}, dimensions={0} | all-to-all | bytes 1048576 | tf_op jit(solution)/shard_map/all_to_all | solution.py:209
  86.3 0.1 reduce_sum.9
  86.5 18.0 %all_to_all.17 = f32[128,8,128]{2,1,0:T(8,128)S(1)} all-to-all(f32[128,8,128]{2,1,0:T(8,128)S(1)} %broadcast_in_dim.2), channel_id=1, replica_groups=mesh['pts'=16,'hrs'=8] {'pts','hrs'}, dimensions={0} | all-to-all | bytes 1048576 | tf_op jit(solution)/shard_map/all_to_all | solution.py:211
  104.5 9.7 %factor_and_apply.1 = (f32[256,2048]{1,0:T(8,128)}, f32[256,512]{1,0:T(8,128)}) custom-call(f32[32,4,8,128]{3,2,1,0:T(8,128)S(1)} %bitcast.5, f32[256,512]{1,0:T(8,128)S(1)} %copy-done, bf16[256,2048]{1,0:T(8,128)(2,1)S(1)} %get-tuple-element.6.high_ref, bf16[256,2048]{1,0:T(8,128)(2,1)S(1)} %get-tuple-element.7.low_ref), custom_call_target="tpu_custom_call" | custom-call | tf_op jit(solution)/shard_map/factor_and_apply/pallas_call | solution.py:188
  (1 shorter events, 0.0 us)
Async XLA Ops:
  0.6 64.5 %copy-start = (f32[256,512]{1,0:T(8,128)S(1)}, f32[256,512]{1,0:T(8,128)}, u32[]{:S(2)}) copy-start(f32[256,512]{1,0:T(8,128)} %probes_ref.1) | copy-start | bytes 1572868

commit v5 on v4

--- a/solution.py
+++ b/solution.py
@@ -106,18 +106,19 @@
                 cols[v, i] = spread(tiles[v][:, first + i : first + i + 1])
         for v in range(t, count):
             tiles[v] = jnp.where(own, jnp.where(lane - first - 8 * (v - t) == sublane, 1.0, 0.0), tiles[v])
+        pivot = spread(cols[t, 0][0:1, :])
         for i in range(PANEL):
             top, s = t + i // 8, i % 8
-            pivot = spread(cols[top, i][s : s + 1, :])
             pivots = pivot if s == 0 else jnp.where(sublane == s, pivot, pivots)
             inverse = 1.0 / pivot
             scaled = {v: cols[v, i] * inverse for v in range(top, count)}
+            if i + 1 < PANEL:
+                u, r = t + (i + 1) // 8, (i + 1) % 8
+                below = spread(cols[u, i][r : r + 1, :])
+                pivot = spread(cols[u, i + 1][r : r + 1, :]) - (below * below) * inverse
             for j in range(i + 1, PANEL):
                 u, r = t + j // 8, j % 8
-                if j == i + 1:
-                    ratio = inverse * spread(cols[u, i][r : r + 1, :])
-                else:
-                    ratio = spread(scaled[u][r : r + 1, :])
+                ratio = inverse * below if j == i + 1 else spread(scaled[u][r : r + 1, :])
                 for v in range(u, count):
                     cols[v, j] = cols[v, j] - cols[v, i] * ratio
             row = spread(tiles[top][s : s + 1, :])
@@ -150,34 +151,34 @@
     return jnp.where(lane <= row, jnp.concatenate(tiles, axis=0), 0.0)
 
 
-def factor_body(moment_ref, probes_ref, high_ref, low_ref, basis_ref, coeffs_ref, out_ref, sems):
+def factor_body(moment_ref, probes_ref, high_ref, low_ref, basis_ref, coeffs_ref, basis_out, coeffs_out, sems):
     n = HALF
     k, pts = high_ref.shape
     moment = jnp.concatenate([moment_ref[:, c].reshape(k, 128) for c in range(moment_ref.shape[1])], axis=1)
     probes = probes_ref[...]
     copies = []
 
-    def write(rows, cols, values):
+    def write(held, ref, rows, cols, values):
         where = (pl.ds(rows, values.shape[0]), pl.ds(cols, values.shape[1]))
-        out_ref[where] = values
-        copies.append(pltpu.make_async_copy(out_ref.at[where], basis_ref.at[where], sems.at[len(copies)]))
+        held[where] = values
+        copies.append(pltpu.make_async_copy(held.at[where], ref.at[where], sems.at[len(copies)]))
         copies[-1].start()
 
     upper = inverse_factor(dot_nt(moment[:n], probes[:n]))
     cross = dot_nn(upper, dot_nt(moment[:n], probes[n:]))
     rest = dot_nt(moment[n:], probes[n:]) - dot_tn(cross, cross)
     basis = dot_split(upper, high_ref[:n, :], low_ref[:n, :])
-    write(0, 0, basis)
+    write(basis_out, basis_ref, 0, 0, basis)
     coeffs = dot_split(upper, *split(moment[:n]))
-    coeffs_ref[:n, :] = coeffs
+    write(coeffs_out, coeffs_ref, 0, 0, coeffs)
     second = high_ref[n:, :].astype(jnp.float32) + low_ref[n:, :].astype(jnp.float32)
     high, low = split(second - dot_split(cross.T, *split(basis)))
     moment_high, moment_low = split(moment[n:] - dot_split(cross.T, *split(coeffs)))
     lower = inverse_factor(rest)
-    coeffs_ref[n:, :] = dot_split(lower, moment_high, moment_low)
     for c in range(0, pts, pts // 2):
         cols = slice(c, c + pts // 2)
-        write(n, c, dot_split(lower, high[:, cols], low[:, cols]))
+        write(basis_out, basis_ref, n, c, dot_split(lower, high[:, cols], low[:, cols]))
+    write(coeffs_out, coeffs_ref, n, 0, dot_split(lower, moment_high, moment_low))
     for copy in copies:
         copy.wait()
 
@@ -189,12 +190,16 @@
         factor_body,
         name="factor_and_apply",
         in_specs=[vmem, vmem, vmem, vmem],
-        out_specs=[pl.BlockSpec(memory_space=pl.ANY), vmem],
+        out_specs=[pl.BlockSpec(memory_space=pl.ANY), pl.BlockSpec(memory_space=pl.ANY)],
         out_shape=[
             jax.ShapeDtypeStruct((k, pts), jnp.float32),
             jax.ShapeDtypeStruct(probes.shape, jnp.float32),
         ],
-        scratch_shapes=[pltpu.VMEM((k, pts), jnp.float32), pltpu.SemaphoreType.DMA((3,))],
+        scratch_shapes=[
+            pltpu.VMEM((k, pts), jnp.float32),
+            pltpu.VMEM(probes.shape, jnp.float32),
+            pltpu.SemaphoreType.DMA((5,)),
+        ],
         compiler_params=pltpu.CompilerParams(vmem_limit_bytes=32 << 20),
     )(moment, probes, high, low)
 

time: 114 us -> 114 us (level)
  no operation moved by 1% of the time
where the time goes in v5:
time: 114 us; the launch traced here: 113 us
  blocking collectives  100 us (88%)
  Pallas kernels  12.4 us (11%)
    all_to_all x1, blocking collectives, on_device(): panels = lax.all_to_all(sent, AXES, split_axis=0, concat_axis=0, tiled=True)  64.5 us
    all_to_all x1, blocking collectives, on_device(): total = lax.all_to_all(total, AXES, split_axis=0, concat_axis=0, tiled=True)  18 us
    all_to_all x1, blocking collectives, on_device(): parts = lax.all_to_all(parts, AXES, split_axis=0, concat_axis=0, tiled=True)  17.6 us
    pallas_call x1, Pallas kernels, factor_and_apply(): pl.pallas_call(factor_body, name='factor_and_apply', in_specs=[vmem, vmem...  8.78 us
    pallas_call x1, Pallas kernels, sketch(): pl.pallas_call(lambda *refs: sketch_body(scale, *refs), name='sketch', in...  3.6 us

profile of v5, /device:TPU:1, one launch (start us, length us, event | category | flops | bytes accessed | tf_op | source)
XLA Modules:
  0.0 113.3 jit_solution(16088724963348459518)
XLA Ops:
  0.6 0.0 copy-start
  0.6 64.5 %all_to_all.15.refs_0_ = f32[128,4,2048]{2,1,0:T(4,128)S(1)} all-to-all(f32[128,4,2048]{2,1,0:T(4,128)} %bitcast.7), channel_id=1, replica_groups=mesh['pts'=16,'hrs'=8] {'pts','hrs'}, dimensions={0} | all-to-all | bytes 8388608 | tf_op jit(solution)/shard_map/all_to_all | solution.py:211
  65.1 0.0 copy-done
  65.1 3.6 %sketch.1 = (bf16[256,2048]{1,0:T(8,128)(2,1)S(1)}, bf16[256,2048]{1,0:T(8,128)(2,1)S(1)}, f32[32,4,8,128]{3,2,1,0:T(8,128)S(1)}) custom-call(f32[128,4,2048]{2,1,0:T(4,128)S(1)} %all_to_all.15.refs_0_, f32[256,512]{1,0:T(8,128)S(1)} %copy-done), custom_call_target="tpu_custom_call" | custom-call | tf_op jit(solution)/shard_map/sketch/pallas_call | solution.py:73
  68.8 17.6 %all_to_all.16 = f32[128,8,128]{2,1,0:T(8,128)S(1)} all-to-all(f32[128,8,128]{2,1,0:T(8,128)S(1)} %bitcast.6), channel_id=1, replica_groups=mesh['pts'=16,'hrs'=8] {'pts','hrs'}, dimensions={0} | all-to-all | bytes 1048576 | tf_op jit(solution)/shard_map/all_to_all | solution.py:214
  86.3 0.1 reduce_sum.9
  86.5 18.0 %all_to_all.17 = f32[128,8,128]{2,1,0:T(8,128)S(1)} all-to-all(f32[128,8,128]{2,1,0:T(8,128)S(1)} %broadcast_in_dim.2), channel_id=1, replica_groups=mesh['pts'=16,'hrs'=8] {'pts','hrs'}, dimensions={0} | all-to-all | bytes 1048576 | tf_op jit(solution)/shard_map/all_to_all | solution.py:216
  104.5 8.8 %factor_and_apply.1 = (f32[256,2048]{1,0:T(8,128)}, f32[256,512]{1,0:T(8,128)}) custom-call(f32[32,4,8,128]{3,2,1,0:T(8,128)S(1)} %bitcast.5, f32[256,512]{1,0:T(8,128)S(1)} %copy-done, bf16[256,2048]{1,0:T(8,128)(2,1)S(1)} %get-tuple-element.6.high_ref, bf16[256,2048]{1,0:T(8,128)(2,1)S(1)} %get-tuple-element.7.low_ref), custom_call_target="tpu_custom_call" | custom-call | tf_op jit(solution)/shard_map/factor_and_apply/pallas_call | solution.py:189
  (1 shorter events, 0.0 us)
Async XLA Ops:
  0.6 64.5 %copy-start = (f32[256,512]{1,0:T(8,128)S(1)}, f32[256,512]{1,0:T(8,128)}, u32[]{:S(2)}) copy-start(f32[256,512]{1,0:T(8,128)} %probes_ref.1) | copy-start | bytes 1572868

commit v6 on v5

--- a/solution.py
+++ b/solution.py
@@ -3,10 +3,13 @@
 from jax import lax
 from jax.experimental import pallas as pl
 from jax.experimental.pallas import tpu as pltpu
+from jax.sharding import Mesh
 from jax.sharding import PartitionSpec as P
 
 highest = lax.Precision.HIGHEST
-AXES = ("pts", "hrs")
+CHIPS = ("pts", "chip")
+AXES = ("pts", "chip", "core")
+SWAP = ((0, 1), (1, 0))
 CHUNK = 512
 HALF = 128
 BLOCK = 32
@@ -43,7 +46,22 @@
     )
 
 
-def sketch_body(scale, panels_ref, probes_ref, high_ref, low_ref, moment_ref, fields_high, fields_low):
+def moment_half(scale, half, high_ref, low_ref, fields_high, fields_low, moment_ref):
+    hours = fields_high.shape[0] // 2
+    rows = pl.ds(pl.multiple_of(half * hours, hours), hours)
+    high = fields_high[rows, :]
+    moment = lax.dot_general(
+        jnp.concatenate([high_ref[...], high_ref[...], low_ref[...]], axis=1),
+        jnp.concatenate([high, fields_low[rows, :], high], axis=1),
+        (((1,), (1,)), ((), ())),
+        preferred_element_type=jnp.float32,
+    )
+    moment = (moment * scale).reshape(-1, 8, hours)
+    for c in range(hours // 128):
+        moment_ref[:, c] = moment[:, :, 128 * c : 128 * c + 128]
+
+
+def sketch_body(scale, panels_ref, probes_ref, high_ref, low_ref, fields_high, fields_low, moment_ref):
     devs, per, pts = panels_ref.shape
     hours = devs * per
     width = min(CHUNK, pts)
@@ -54,38 +72,37 @@
         fields_high[:, cols] = high
         fields_low[:, cols] = low
         high_ref[:, cols], low_ref[:, cols] = split(dot_split(probes, high, low))
-    high, low = high_ref[...], low_ref[...]
-    moment = lax.dot_general(
-        jnp.concatenate([high, high, low], axis=1),
-        jnp.concatenate([fields_high[...], fields_low[...], fields_high[...]], axis=1),
-        (((1,), (1,)), ((), ())),
-        preferred_element_type=jnp.float32,
-    )
-    moment = (moment * scale).reshape(-1, 8, hours)
-    for c in range(hours // 128):
-        moment_ref[:, c] = moment[:, :, 128 * c : 128 * c + 128]
+    moment_half(scale, 1 - lax.axis_index("core"), high_ref, low_ref, fields_high, fields_low, moment_ref)
+
+
+def own_body(scale, high_ref, low_ref, fields_high, fields_low, moment_ref):
+    moment_half(scale, lax.axis_index("core"), high_ref, low_ref, fields_high, fields_low, moment_ref)
 
 
 def sketch(panels, probes, scale):
     devs, per, pts = panels.shape
     k, hours = probes.shape
     vmem = pl.BlockSpec(memory_space=pltpu.VMEM)
-    return pl.pallas_call(
+    params = pltpu.CompilerParams(vmem_limit_bytes=32 << 20)
+    moment = jax.ShapeDtypeStruct((k // 8, hours // 256, 8, 128), jnp.float32)
+    parts = [jax.ShapeDtypeStruct((n, pts), jnp.bfloat16) for n in (k, k, hours, hours)]
+    *held, other = pl.pallas_call(
         lambda *refs: sketch_body(scale, *refs),
         name="sketch",
         in_specs=[vmem, vmem],
-        out_specs=[vmem, vmem, vmem],
-        out_shape=[
-            jax.ShapeDtypeStruct((k, pts), jnp.bfloat16),
-            jax.ShapeDtypeStruct((k, pts), jnp.bfloat16),
-            jax.ShapeDtypeStruct((k // 8, hours // 128, 8, 128), jnp.float32),
-        ],
-        scratch_shapes=[
-            pltpu.VMEM((hours, pts), jnp.bfloat16),
-            pltpu.VMEM((hours, pts), jnp.bfloat16),
-        ],
-        compiler_params=pltpu.CompilerParams(vmem_limit_bytes=32 << 20),
+        out_specs=[vmem] * 5,
+        out_shape=[*parts, moment],
+        compiler_params=params,
     )(panels, probes)
+    own = pl.pallas_call(
+        lambda *refs: own_body(scale, *refs),
+        name="own_moment",
+        in_specs=[vmem] * 4,
+        out_specs=vmem,
+        out_shape=moment,
+        compiler_params=params,
+    )(*held)
+    return held[0], held[1], own, other
 
 
 def spread(x):
@@ -151,10 +168,15 @@
     return jnp.where(lane <= row, jnp.concatenate(tiles, axis=0), 0.0)
 
 
-def factor_body(moment_ref, probes_ref, high_ref, low_ref, basis_ref, coeffs_ref, basis_out, coeffs_out, sems):
+def factor_body(own_ref, other_ref, probes_ref, high_ref, low_ref, basis_ref, coeffs_ref, basis_out, coeffs_out, sems):
     n = HALF
     k, pts = high_ref.shape
-    moment = jnp.concatenate([moment_ref[:, c].reshape(k, 128) for c in range(moment_ref.shape[1])], axis=1)
+    own, other = (
+        jnp.concatenate([ref[:, c].reshape(k, 128) for c in range(ref.shape[1])], axis=1)
+        for ref in (own_ref, other_ref)
+    )
+    first = lax.axis_index("core") == 0
+    moment = jnp.concatenate([jnp.where(first, own, other), jnp.where(first, other, own)], axis=1)
     probes = probes_ref[...]
     copies = []
 
@@ -183,13 +205,13 @@
         copy.wait()
 
 
-def factor_and_apply(moment, probes, high, low):
+def factor_and_apply(own, other, probes, high, low):
     k, pts = high.shape
     vmem = pl.BlockSpec(memory_space=pltpu.VMEM)
     return pl.pallas_call(
         factor_body,
         name="factor_and_apply",
-        in_specs=[vmem, vmem, vmem, vmem],
+        in_specs=[vmem] * 5,
         out_specs=[pl.BlockSpec(memory_space=pl.ANY), pl.BlockSpec(memory_space=pl.ANY)],
         out_shape=[
             jax.ShapeDtypeStruct((k, pts), jnp.float32),
@@ -201,27 +223,30 @@
             pltpu.SemaphoreType.DMA((5,)),
         ],
         compiler_params=pltpu.CompilerParams(vmem_limit_bytes=32 << 20),
-    )(moment, probes, high, low)
+    )(own, other, probes, high, low)
 
 
 def on_device(fields, probes):
-    devices = lax.axis_size("pts") * lax.axis_size("hrs")
+    chips = lax.axis_size("pts") * lax.axis_size("chip")
+    devices = chips * lax.axis_size("core")
     per, n_points = fields.shape
     sent = fields.reshape(per, devices, n_points // devices).transpose(1, 0, 2)
     panels = lax.all_to_all(sent, AXES, split_axis=0, concat_axis=0, tiled=True)
-    high, low, moment = sketch(panels, probes, 1.0 / n_points)
-    parts = moment.reshape(devices, -1, 128)
-    parts = lax.all_to_all(parts, AXES, split_axis=0, concat_axis=0, tiled=True)
+    high, low, own, other = sketch(panels, probes, 1.0 / n_points)
+    parts = (own + lax.ppermute(other, "core", SWAP)).reshape(chips, -1, 128)
+    parts = lax.all_to_all(parts, CHIPS, split_axis=0, concat_axis=0, tiled=True)
     total = jnp.broadcast_to(jnp.sum(parts, axis=0)[None], parts.shape)
-    total = lax.all_to_all(total, AXES, split_axis=0, concat_axis=0, tiled=True)
-    basis_rows, coeffs = factor_and_apply(total.reshape(moment.shape), probes, high, low)
+    total = lax.all_to_all(total, CHIPS, split_axis=0, concat_axis=0, tiled=True).reshape(own.shape)
+    basis_rows, coeffs = factor_and_apply(total, lax.ppermute(total, "core", SWAP), probes, high, low)
     return (basis_rows, coeffs)
 
 
 def solution(mesh):
+    pts, hrs = mesh.devices.shape
+    cores = Mesh(mesh.devices.reshape(pts, hrs // 2, 2), AXES)
     return jax.shard_map(
         on_device,
-        mesh=mesh,
+        mesh=cores,
         in_specs=(P(AXES, None), P()),
         out_specs=(P(None, AXES), P()),
         check_vma=False,

time: 114 us -> 113 us (level)
  blocking collectives: 100 us -> 92.1 us
  starting transfers between devices: 0 us -> 4.06 us
  Pallas kernels: 12.4 us -> 13.9 us
  waiting for transfers between devices: 0 us -> 1.31 us
    all_to_all x2, blocking collectives: 35.6 us -> 27.6 us  [the longest x1 13.8 us: on_device(): lax.all_to_all(parts, CHIPS, split_axis=0, concat_axis=0, tiled=True)]
    ppermute x0 -> x2, starting transfers between devices: none -> 4.06 us  [the longest x1 3.05 us: on_device(): lax.ppermute(total, 'core', SWAP)]
    ppermute x0 -> x2, waiting for transfers between devices: none -> 1.31 us  [the longest x1 1.16 us: on_device(): lax.ppermute(total, 'core', SWAP)]
    pallas_call x1 -> x2, Pallas kernels: 8.78 us -> 9.78 us  [the longest x1 8.76 us: factor_and_apply(): pl.pallas_call(factor_body, name='factor_and_apply', in_specs=[vmem] * 5,...]
  transfers between devices with their start and end apart: 0 -> 2, of which waited for: 0 -> 2; matrix products, arithmetic and copies ran while one was open for 0% -> 0% of each run, Pallas kernels for 0% -> 1%
where the time goes in v6:
time: 113 us; the launch traced here: 112 us
  blocking collectives  92.1 us (82%)
  Pallas kernels  13.9 us (12%)
  starting transfers between devices  4.06 us (4%)
  waiting for transfers between devices  1.31 us (1%)
    all_to_all x1, blocking collectives, on_device(): panels = lax.all_to_all(sent, AXES, split_axis=0, concat_axis=0, tiled=True)  64.5 us
    all_to_all x1, blocking collectives, on_device(): lax.all_to_all(parts, CHIPS, split_axis=0, concat_axis=0, tiled=True)  13.8 us
    all_to_all x1, blocking collectives, on_device(): lax.all_to_all(total, CHIPS, split_axis=0, concat_axis=0, tiled=True)  13.8 us
    pallas_call x1, Pallas kernels, factor_and_apply(): pl.pallas_call(factor_body, name='factor_and_apply', in_specs=[vmem] * 5,...  8.76 us
    pallas_call x1, Pallas kernels, sketch(): pl.pallas_call(lambda *refs: sketch_body(scale, *refs), name='sketch', in...  4.09 us
    ppermute x1, starting transfers between devices, on_device(): lax.ppermute(total, 'core', SWAP)  3.05 us
  transfers between devices with their start and end apart: 2, of which 2 were waited for; matrix products, arithmetic and copies ran while one was open for 0% of the time, Pallas kernels for 1%

profile of v6, /device:TPU:1, one launch (start us, length us, event | category | flops | bytes accessed | tf_op | source)
XLA Modules:
  0.0 112.3 jit_solution(2763058204539562727)
XLA Ops:
  0.6 0.0 copy-start
  0.6 64.5 %all_to_all.15.refs_0_ = f32[128,4,2048]{2,1,0:T(4,128)S(1)} all-to-all(f32[128,4,2048]{2,1,0:T(4,128)} %bitcast.7), channel_id=1, replica_groups=mesh['pts'=16,'chip'=4,'core'=2] {'pts','chip','core'}, dimensions={0} | all-to-all | bytes 8388608 | tf_op jit(solution)/shard_map/all_to_all | solution.py:234
  65.1 0.0 copy-done
  65.1 4.1 %sketch.1 = (bf16[256,2048]{1,0:T(8,128)(2,1)S(1)}, bf16[256,2048]{1,0:T(8,128)(2,1)S(1)}, bf16[512,2048]{1,0:T(8,128)(2,1)S(1)}, bf16[512,2048]{1,0:T(8,128)(2,1)S(1)}, f32[32,2,8,128]{3,2,1,0:T(8,128)S(1)}) custom-call(f32[128,4,2048]{2,1,0:T(4,128)S(1)} %all_to_all.15.refs_0_, f32[256,512]{1,0:T(8,128)S(1)} %copy-done), custom_call_target="tpu_custom_call" | custom-call | tf_op jit(solution)/shard_map/sketch/pallas_call | solution.py:89
  69.3 1.0 collective-permute-start
  70.3 1.0 own_moment.1
  71.3 0.1 collective-permute-done
  71.5 13.8 %all_to_all.16 = f32[64,8,128]{2,1,0:T(8,128)S(1)} all-to-all(f32[64,8,128]{2,1,0:T(8,128)S(1)} %bitcast.8), channel_id=1, replica_groups=mesh['pts'=16,'chip'=4,'core'=2] {'pts','chip'}, dimensions={0} | all-to-all | bytes 524288 | tf_op jit(solution)/shard_map/all_to_all | solution.py:237
  85.3 0.1 reduce_sum.9
  85.4 13.8 %all_to_all.17 = f32[64,8,128]{2,1,0:T(8,128)S(1)} all-to-all(f32[64,8,128]{2,1,0:T(8,128)S(1)} %broadcast_in_dim.2), channel_id=1, replica_groups=mesh['pts'=16,'chip'=4,'core'=2] {'pts','chip'}, dimensions={0} | all-to-all | bytes 524288 | tf_op jit(solution)/shard_map/all_to_all | solution.py:239
  99.2 3.0 %collective-permute-start.1 = (f32[32,2,8,128]{3,2,1,0:T(8,128)S(1)}, f32[32,2,8,128]{3,2,1,0:T(8,128)S(1)}, u32[]{:S(2)}, u32[]{:S(2)}) collective-permute-start(f32[32,2,8,128]{3,2,1,0:T(8,128)S(1)} %bitcast.5), channel_id=1, source_target_pairs={{0,1},{1,0},{2,3},{3,2},{4,5},{5,4},{6,7},{7,6},{8,9},{9,8},{10,11... | collective-permute-start | bytes 786440 | tf_op jit(solution)/shard_map/ppermute | solution.py:240
  102.2 1.2 %collective-permute-done.1.other_ref = f32[32,2,8,128]{3,2,1,0:T(8,128)S(1)} collective-permute-done((f32[32,2,8,128]{3,2,1,0:T(8,128)S(1)}, f32[32,2,8,128]{3,2,1,0:T(8,128)S(1)}, u32[]{:S(2)}, u32[]{:S(2)}) %collective-permute-start.1) | collective-permute-done | bytes 262176 | tf_op jit(solution)/shard_map/ppermute | solution.py:240
  103.4 8.8 %factor_and_apply.1 = (f32[256,2048]{1,0:T(8,128)}, f32[256,512]{1,0:T(8,128)}) custom-call(f32[32,2,8,128]{3,2,1,0:T(8,128)S(1)} %bitcast.6, f32[32,2,8,128]{3,2,1,0:T(8,128)S(1)} %collective-permute-done.1.other_ref, f32[256,512]{1,0:T(8,128)S(1)} %copy-done, bf16[256,2048]{1,0:T(8,128)(2,1)S(1)} %get-tuple-element.7.refs_0_.high_ref, ...), custom_call_target="tpu_custom_call" | custom-call | tf_op jit(solution)/shard_map/factor_and_apply/pallas_call | solution.py:211
  (2 shorter events, 0.1 us)
Async XLA Ops:
  0.6 64.5 %copy-start = (f32[256,512]{1,0:T(8,128)S(1)}, f32[256,512]{1,0:T(8,128)}, u32[]{:S(2)}) copy-start(f32[256,512]{1,0:T(8,128)} %probes_ref.1) | copy-start | bytes 1572868
  69.3 2.2 %collective-permute-start = (f32[32,2,8,128]{3,2,1,0:T(8,128)S(1)}, f32[32,2,8,128]{3,2,1,0:T(8,128)S(1)}, u32[]{:S(2)}, u32[]{:S(2)}) collective-permute-start(f32[32,2,8,128]{3,2,1,0:T(8,128)S(1)} %get-tuple-element.11), channel_id=1, source_target_pairs={{0,1},{1,0},{2,3},{3,2},{4,5},{5,4},{6,7},{7,6},{8,9},{9,8},{10,11... | collective-permute-start | bytes 786440 | tf_op jit(solution)/shard_map/ppermute | solution.py:236
  99.2 4.2 %collective-permute-start.1 = (f32[32,2,8,128]{3,2,1,0:T(8,128)S(1)}, f32[32,2,8,128]{3,2,1,0:T(8,128)S(1)}, u32[]{:S(2)}, u32[]{:S(2)}) collective-permute-start(f32[32,2,8,128]{3,2,1,0:T(8,128)S(1)} %bitcast.5), channel_id=1, source_target_pairs={{0,1},{1,0},{2,3},{3,2},{4,5},{5,4},{6,7},{7,6},{8,9},{9,8},{10,11... | collective-permute-start | bytes 786440 | tf_op jit(solution)/shard_map/ppermute | solution.py:240

commit v7 on v6

--- a/solution.py
+++ b/solution.py
@@ -12,8 +12,9 @@
 SWAP = ((0, 1), (1, 0))
 CHUNK = 512
 HALF = 128
-BLOCK = 32
+BLOCK = 64
 PANEL = 16
+PIECES = 4
 
 
 def dot_nn(left, right):
@@ -46,22 +47,7 @@
     )
 
 
-def moment_half(scale, half, high_ref, low_ref, fields_high, fields_low, moment_ref):
-    hours = fields_high.shape[0] // 2
-    rows = pl.ds(pl.multiple_of(half * hours, hours), hours)
-    high = fields_high[rows, :]
-    moment = lax.dot_general(
-        jnp.concatenate([high_ref[...], high_ref[...], low_ref[...]], axis=1),
-        jnp.concatenate([high, fields_low[rows, :], high], axis=1),
-        (((1,), (1,)), ((), ())),
-        preferred_element_type=jnp.float32,
-    )
-    moment = (moment * scale).reshape(-1, 8, hours)
-    for c in range(hours // 128):
-        moment_ref[:, c] = moment[:, :, 128 * c : 128 * c + 128]
-
-
-def sketch_body(scale, panels_ref, probes_ref, high_ref, low_ref, fields_high, fields_low, moment_ref):
+def sketch_body(scale, panels_ref, probes_ref, high_ref, low_ref, own_ref, other_ref, fields_high, fields_low):
     devs, per, pts = panels_ref.shape
     hours = devs * per
     width = min(CHUNK, pts)
@@ -72,37 +58,37 @@
         fields_high[:, cols] = high
         fields_low[:, cols] = low
         high_ref[:, cols], low_ref[:, cols] = split(dot_split(probes, high, low))
-    moment_half(scale, 1 - lax.axis_index("core"), high_ref, low_ref, fields_high, fields_low, moment_ref)
-
-
-def own_body(scale, high_ref, low_ref, fields_high, fields_low, moment_ref):
-    moment_half(scale, lax.axis_index("core"), high_ref, low_ref, fields_high, fields_low, moment_ref)
+    high, low = high_ref[...], low_ref[...]
+    moment = lax.dot_general(
+        jnp.concatenate([high, high, low], axis=1),
+        jnp.concatenate([fields_high[...], fields_low[...], fields_high[...]], axis=1),
+        (((1,), (1,)), ((), ())),
+        preferred_element_type=jnp.float32,
+    )
+    moment = (moment * scale).reshape(-1, 8, hours)
+    first = lax.axis_index("core") == 0
+    for c in range(hours // 256):
+        left = moment[:, :, 128 * c : 128 * c + 128]
+        right = moment[:, :, hours // 2 + 128 * c : hours // 2 + 128 * c + 128]
+        own_ref[:, c] = jnp.where(first, left, right)
+        other_ref[:, c] = jnp.where(first, right, left)
 
 
 def sketch(panels, probes, scale):
     devs, per, pts = panels.shape
     k, hours = probes.shape
     vmem = pl.BlockSpec(memory_space=pltpu.VMEM)
-    params = pltpu.CompilerParams(vmem_limit_bytes=32 << 20)
-    moment = jax.ShapeDtypeStruct((k // 8, hours // 256, 8, 128), jnp.float32)
-    parts = [jax.ShapeDtypeStruct((n, pts), jnp.bfloat16) for n in (k, k, hours, hours)]
-    *held, other = pl.pallas_call(
+    part = jax.ShapeDtypeStruct((k, pts), jnp.bfloat16)
+    half = jax.ShapeDtypeStruct((k // 8, hours // 256, 8, 128), jnp.float32)
+    return pl.pallas_call(
         lambda *refs: sketch_body(scale, *refs),
         name="sketch",
         in_specs=[vmem, vmem],
-        out_specs=[vmem] * 5,
-        out_shape=[*parts, moment],
-        compiler_params=params,
+        out_specs=[vmem] * 4,
+        out_shape=[part, part, half, half],
+        scratch_shapes=[pltpu.VMEM((hours, pts), jnp.bfloat16), pltpu.VMEM((hours, pts), jnp.bfloat16)],
+        compiler_params=pltpu.CompilerParams(vmem_limit_bytes=32 << 20),
     )(panels, probes)
-    own = pl.pallas_call(
-        lambda *refs: own_body(scale, *refs),
-        name="own_moment",
-        in_specs=[vmem] * 4,
-        out_specs=vmem,
-        out_shape=moment,
-        compiler_params=params,
-    )(*held)
-    return held[0], held[1], own, other
 
 
 def spread(x):
@@ -197,8 +183,8 @@
     high, low = split(second - dot_split(cross.T, *split(basis)))
     moment_high, moment_low = split(moment[n:] - dot_split(cross.T, *split(coeffs)))
     lower = inverse_factor(rest)
-    for c in range(0, pts, pts // 2):
-        cols = slice(c, c + pts // 2)
+    for c in range(0, pts, pts // PIECES):
+        cols = slice(c, c + pts // PIECES)
         write(basis_out, basis_ref, n, c, dot_split(lower, high[:, cols], low[:, cols]))
     write(coeffs_out, coeffs_ref, n, 0, dot_split(lower, moment_high, moment_low))
     for copy in copies:
@@ -220,7 +206,7 @@
         scratch_shapes=[
             pltpu.VMEM((k, pts), jnp.float32),
             pltpu.VMEM(probes.shape, jnp.float32),
-            pltpu.SemaphoreType.DMA((5,)),
+            pltpu.SemaphoreType.DMA((PIECES + 3,)),
         ],
         compiler_params=pltpu.CompilerParams(vmem_limit_bytes=32 << 20),
     )(own, other, probes, high, low)

time: 113 us -> 112 us (level)
  Pallas kernels: 13.9 us -> 12 us
  transfers between devices with their start and end apart: 2 -> 2, of which waited for: 2 -> 2; matrix products, arithmetic and copies ran while one was open for 0% -> 0% of each run, Pallas kernels for 1% -> 0%
where the time goes in v7:
time: 112 us; the launch traced here: 111 us
  blocking collectives  92.1 us (82%)
  Pallas kernels  12 us (11%)
  starting transfers between devices  4.07 us (4%)
  waiting for transfers between devices  2.32 us (2%)
    all_to_all x1, blocking collectives, on_device(): panels = lax.all_to_all(sent, AXES, split_axis=0, concat_axis=0, tiled=True)  64.5 us
    all_to_all x1, blocking collectives, on_device(): lax.all_to_all(parts, CHIPS, split_axis=0, concat_axis=0, tiled=True)  13.8 us
    all_to_all x1, blocking collectives, on_device(): lax.all_to_all(total, CHIPS, split_axis=0, concat_axis=0, tiled=True)  13.8 us
    pallas_call x1, Pallas kernels, factor_and_apply(): pl.pallas_call(factor_body, name='factor_and_apply', in_specs=[vmem] * 5,...  8.4 us
    pallas_call x1, Pallas kernels, sketch(): pl.pallas_call(lambda *refs: sketch_body(scale, *refs), name='sketch', in...  3.6 us
    ppermute x1, starting transfers between devices, on_device(): lax.ppermute(total, 'core', SWAP)  3.05 us
  transfers between devices with their start and end apart: 2, of which 2 were waited for; matrix products, arithmetic and copies ran while one was open for 0% of the time, Pallas kernels for 0%

profile of v7, /device:TPU:1, one launch (start us, length us, event | category | flops | bytes accessed | tf_op | source)
XLA Modules:
  0.0 111.4 jit_solution(10263249057258984571)
XLA Ops:
  0.6 0.0 copy-start
  0.6 64.5 %all_to_all.15.refs_0_ = f32[128,4,2048]{2,1,0:T(4,128)S(1)} all-to-all(f32[128,4,2048]{2,1,0:T(4,128)} %bitcast.7), channel_id=1, replica_groups=mesh['pts'=16,'chip'=4,'core'=2] {'pts','chip','core'}, dimensions={0} | all-to-all | bytes 8388608 | tf_op jit(solution)/shard_map/all_to_all | solution.py:220
  65.1 0.0 copy-done
  65.1 3.6 %sketch.1 = (bf16[256,2048]{1,0:T(8,128)(2,1)S(1)}, bf16[256,2048]{1,0:T(8,128)(2,1)S(1)}, f32[32,2,8,128]{3,2,1,0:T(8,128)S(1)}, f32[32,2,8,128]{3,2,1,0:T(8,128)S(1)}) custom-call(f32[128,4,2048]{2,1,0:T(4,128)S(1)} %all_to_all.15.refs_0_, f32[256,512]{1,0:T(8,128)S(1)} %copy-done), custom_call_target="tpu_custom_call" | custom-call | tf_op jit(solution)/shard_map/sketch/pallas_call | solution.py:83
  68.8 1.0 collective-permute-start
  69.8 1.2 %collective-permute-done = f32[32,2,8,128]{3,2,1,0:T(8,128)S(1)} collective-permute-done((f32[32,2,8,128]{3,2,1,0:T(8,128)S(1)}, f32[32,2,8,128]{3,2,1,0:T(8,128)S(1)}, u32[]{:S(2)}, u32[]{:S(2)}) %collective-permute-start) | collective-permute-done | bytes 262176 | tf_op jit(solution)/shard_map/ppermute | solution.py:222
  71.0 13.8 %all_to_all.16 = f32[64,8,128]{2,1,0:T(8,128)S(1)} all-to-all(f32[64,8,128]{2,1,0:T(8,128)S(1)} %bitcast.8), channel_id=1, replica_groups=mesh['pts'=16,'chip'=4,'core'=2] {'pts','chip'}, dimensions={0} | all-to-all | bytes 524288 | tf_op jit(solution)/shard_map/all_to_all | solution.py:223
  84.8 0.1 reduce_sum.9
  84.9 13.8 %all_to_all.17 = f32[64,8,128]{2,1,0:T(8,128)S(1)} all-to-all(f32[64,8,128]{2,1,0:T(8,128)S(1)} %broadcast_in_dim.2), channel_id=1, replica_groups=mesh['pts'=16,'chip'=4,'core'=2] {'pts','chip'}, dimensions={0} | all-to-all | bytes 524288 | tf_op jit(solution)/shard_map/all_to_all | solution.py:225
  98.7 3.0 %collective-permute-start.1 = (f32[32,2,8,128]{3,2,1,0:T(8,128)S(1)}, f32[32,2,8,128]{3,2,1,0:T(8,128)S(1)}, u32[]{:S(2)}, u32[]{:S(2)}) collective-permute-start(f32[32,2,8,128]{3,2,1,0:T(8,128)S(1)} %bitcast.5), channel_id=1, source_target_pairs={{0,1},{1,0},{2,3},{3,2},{4,5},{5,4},{6,7},{7,6},{8,9},{9,8},{10,11... | collective-permute-start | bytes 786440 | tf_op jit(solution)/shard_map/ppermute | solution.py:226
  101.7 1.2 %collective-permute-done.1.other_ref = f32[32,2,8,128]{3,2,1,0:T(8,128)S(1)} collective-permute-done((f32[32,2,8,128]{3,2,1,0:T(8,128)S(1)}, f32[32,2,8,128]{3,2,1,0:T(8,128)S(1)}, u32[]{:S(2)}, u32[]{:S(2)}) %collective-permute-start.1) | collective-permute-done | bytes 262176 | tf_op jit(solution)/shard_map/ppermute | solution.py:226
  102.9 8.4 %factor_and_apply.1 = (f32[256,2048]{1,0:T(8,128)}, f32[256,512]{1,0:T(8,128)}) custom-call(f32[32,2,8,128]{3,2,1,0:T(8,128)S(1)} %bitcast.6, f32[32,2,8,128]{3,2,1,0:T(8,128)S(1)} %collective-permute-done.1.other_ref, f32[256,512]{1,0:T(8,128)S(1)} %copy-done, bf16[256,2048]{1,0:T(8,128)(2,1)S(1)} %get-tuple-element.8.high_ref, ...), custom_call_target="tpu_custom_call" | custom-call | tf_op jit(solution)/shard_map/factor_and_apply/pallas_call | solution.py:197
  (2 shorter events, 0.1 us)
Async XLA Ops:
  0.6 64.5 %copy-start = (f32[256,512]{1,0:T(8,128)S(1)}, f32[256,512]{1,0:T(8,128)}, u32[]{:S(2)}) copy-start(f32[256,512]{1,0:T(8,128)} %probes_ref.1) | copy-start | bytes 1572868
  68.8 2.2 %collective-permute-start = (f32[32,2,8,128]{3,2,1,0:T(8,128)S(1)}, f32[32,2,8,128]{3,2,1,0:T(8,128)S(1)}, u32[]{:S(2)}, u32[]{:S(2)}) collective-permute-start(f32[32,2,8,128]{3,2,1,0:T(8,128)S(1)} %get-tuple-element.7), channel_id=1, source_target_pairs={{0,1},{1,0},{2,3},{3,2},{4,5},{5,4},{6,7},{7,6},{8,9},{9,8},{10,11... | collective-permute-start | bytes 786440 | tf_op jit(solution)/shard_map/ppermute | solution.py:222
  98.7 4.2 %collective-permute-start.1 = (f32[32,2,8,128]{3,2,1,0:T(8,128)S(1)}, f32[32,2,8,128]{3,2,1,0:T(8,128)S(1)}, u32[]{:S(2)}, u32[]{:S(2)}) collective-permute-start(f32[32,2,8,128]{3,2,1,0:T(8,128)S(1)} %bitcast.5), channel_id=1, source_target_pairs={{0,1},{1,0},{2,3},{3,2},{4,5},{5,4},{6,7},{7,6},{8,9},{9,8},{10,11... | collective-permute-start | bytes 786440 | tf_op jit(solution)/shard_map/ppermute | solution.py:226

commit v8 on v7

--- a/solution.py
+++ b/solution.py
@@ -154,16 +154,37 @@
     return jnp.where(lane <= row, jnp.concatenate(tiles, axis=0), 0.0)
 
 
-def factor_body(own_ref, other_ref, probes_ref, high_ref, low_ref, basis_ref, coeffs_ref, basis_out, coeffs_out, sems):
+def join(ref):
+    return jnp.concatenate([ref[:, c].reshape(-1, 128) for c in range(ref.shape[1])], axis=1)
+
+
+def gram_body(own_ref, probes_ref, gram_ref):
+    half = probes_ref.shape[1] // 2
+    first = lax.axis_index("core") == 0
+    gram_ref[...] = dot_nt(join(own_ref), jnp.where(first, probes_ref[:, :half], probes_ref[:, half:]))
+
+
+def own_gram(own, probes):
+    k = probes.shape[0]
+    vmem = pl.BlockSpec(memory_space=pltpu.VMEM)
+    return pl.pallas_call(
+        gram_body,
+        name="own_gram",
+        in_specs=[vmem, vmem],
+        out_specs=vmem,
+        out_shape=jax.ShapeDtypeStruct((k, k), jnp.float32),
+        compiler_params=pltpu.CompilerParams(vmem_limit_bytes=32 << 20),
+    )(own, probes)
+
+
+def factor_body(gram_ref, own_ref, other_ref, probes_ref, high_ref, low_ref, basis_ref, coeffs_ref, basis_out, coeffs_out, sems):
     n = HALF
     k, pts = high_ref.shape
-    own, other = (
-        jnp.concatenate([ref[:, c].reshape(k, 128) for c in range(ref.shape[1])], axis=1)
-        for ref in (own_ref, other_ref)
-    )
+    own, other = join(own_ref), join(other_ref)
     first = lax.axis_index("core") == 0
     moment = jnp.concatenate([jnp.where(first, own, other), jnp.where(first, other, own)], axis=1)
-    probes = probes_ref[...]
+    half = probes_ref.shape[1] // 2
+    probes = jnp.where(first, probes_ref[:, half:], probes_ref[:, :half])
     copies = []
 
     def write(held, ref, rows, cols, values):
@@ -172,9 +193,9 @@
         copies.append(pltpu.make_async_copy(held.at[where], ref.at[where], sems.at[len(copies)]))
         copies[-1].start()
 
-    upper = inverse_factor(dot_nt(moment[:n], probes[:n]))
-    cross = dot_nn(upper, dot_nt(moment[:n], probes[n:]))
-    rest = dot_nt(moment[n:], probes[n:]) - dot_tn(cross, cross)
+    upper = inverse_factor(gram_ref[:n, :n] + dot_nt(other[:n], probes[:n]))
+    cross = dot_nn(upper, gram_ref[:n, n:] + dot_nt(other[:n], probes[n:]))
+    rest = gram_ref[n:, n:] + dot_nt(other[n:], probes[n:]) - dot_tn(cross, cross)
     basis = dot_split(upper, high_ref[:n, :], low_ref[:n, :])
     write(basis_out, basis_ref, 0, 0, basis)
     coeffs = dot_split(upper, *split(moment[:n]))
@@ -191,13 +212,13 @@
         copy.wait()
 
 
-def factor_and_apply(own, other, probes, high, low):
+def factor_and_apply(gram, own, other, probes, high, low):
     k, pts = high.shape
     vmem = pl.BlockSpec(memory_space=pltpu.VMEM)
     return pl.pallas_call(
         factor_body,
         name="factor_and_apply",
-        in_specs=[vmem] * 5,
+        in_specs=[vmem] * 6,
         out_specs=[pl.BlockSpec(memory_space=pl.ANY), pl.BlockSpec(memory_space=pl.ANY)],
         out_shape=[
             jax.ShapeDtypeStruct((k, pts), jnp.float32),
@@ -209,7 +230,7 @@
             pltpu.SemaphoreType.DMA((PIECES + 3,)),
         ],
         compiler_params=pltpu.CompilerParams(vmem_limit_bytes=32 << 20),
-    )(own, other, probes, high, low)
+    )(gram, own, other, probes, high, low)
 
 
 def on_device(fields, probes):
@@ -223,7 +244,8 @@
     parts = lax.all_to_all(parts, CHIPS, split_axis=0, concat_axis=0, tiled=True)
     total = jnp.broadcast_to(jnp.sum(parts, axis=0)[None], parts.shape)
     total = lax.all_to_all(total, CHIPS, split_axis=0, concat_axis=0, tiled=True).reshape(own.shape)
-    basis_rows, coeffs = factor_and_apply(total, lax.ppermute(total, "core", SWAP), probes, high, low)
+    swapped = lax.ppermute(total, "core", SWAP)
+    basis_rows, coeffs = factor_and_apply(own_gram(total, probes), total, swapped, probes, high, low)
     return (basis_rows, coeffs)
 
 

time: 112 us -> 111 us (level)
    pallas_call x1 -> x2, Pallas kernels: 8.4 us -> 8.4 us  [the longest x1 7.99 us: factor_and_apply(): pl.pallas_call(factor_body, name='factor_and_apply', in_specs=[vmem] * 6,...]
where the time goes in v8:
time: 111 us
  blocking collectives  92.1 us (83%)
  Pallas kernels  12 us (11%)
  starting transfers between devices  4.07 us (4%)
  waiting for transfers between devices  1.9 us (2%)
    all_to_all x1, blocking collectives, on_device(): panels = lax.all_to_all(sent, AXES, split_axis=0, concat_axis=0, tiled=True)  64.5 us
    all_to_all x1, blocking collectives, on_device(): lax.all_to_all(parts, CHIPS, split_axis=0, concat_axis=0, tiled=True)  13.8 us
    all_to_all x1, blocking collectives, on_device(): lax.all_to_all(total, CHIPS, split_axis=0, concat_axis=0, tiled=True)  13.8 us
    pallas_call x1, Pallas kernels, factor_and_apply(): pl.pallas_call(factor_body, name='factor_and_apply', in_specs=[vmem] * 6,...  7.99 us
    pallas_call x1, Pallas kernels, sketch(): pl.pallas_call(lambda *refs: sketch_body(scale, *refs), name='sketch', in...  3.6 us
    ppermute x1, starting transfers between devices, on_device(): swapped = lax.ppermute(total, 'core', SWAP)  3.05 us
  transfers between devices with their start and end apart: 2, of which 2 were waited for; matrix products, arithmetic and copies ran while one was open for 0% of the time, Pallas kernels for 0%

profile of v8, /device:TPU:1, one launch (start us, length us, event | category | flops | bytes accessed | tf_op | source)
XLA Modules:
  0.0 111.0 jit_solution(2993938002312915293)
XLA Ops:
  0.6 0.0 copy-start
  0.6 64.5 %all_to_all.15.refs_0_ = f32[128,4,2048]{2,1,0:T(4,128)S(1)} all-to-all(f32[128,4,2048]{2,1,0:T(4,128)} %bitcast.8), channel_id=1, replica_groups=mesh['pts'=16,'chip'=4,'core'=2] {'pts','chip','core'}, dimensions={0} | all-to-all | bytes 8388608 | tf_op jit(solution)/shard_map/all_to_all | solution.py:241
  65.1 0.0 copy-done
  65.1 3.6 %sketch.1 = (bf16[256,2048]{1,0:T(8,128)(2,1)S(1)}, bf16[256,2048]{1,0:T(8,128)(2,1)S(1)}, f32[32,2,8,128]{3,2,1,0:T(8,128)S(1)}, f32[32,2,8,128]{3,2,1,0:T(8,128)S(1)}) custom-call(f32[128,4,2048]{2,1,0:T(4,128)S(1)} %all_to_all.15.refs_0_, f32[256,512]{1,0:T(8,128)S(1)} %copy-done), custom_call_target="tpu_custom_call" | custom-call | tf_op jit(solution)/shard_map/sketch/pallas_call | solution.py:83
  68.8 1.0 collective-permute-start
  69.8 1.2 %collective-permute-done = f32[32,2,8,128]{3,2,1,0:T(8,128)S(1)} collective-permute-done((f32[32,2,8,128]{3,2,1,0:T(8,128)S(1)}, f32[32,2,8,128]{3,2,1,0:T(8,128)S(1)}, u32[]{:S(2)}, u32[]{:S(2)}) %collective-permute-start) | collective-permute-done | bytes 262176 | tf_op jit(solution)/shard_map/ppermute | solution.py:243
  71.0 13.8 %all_to_all.16 = f32[64,8,128]{2,1,0:T(8,128)S(1)} all-to-all(f32[64,8,128]{2,1,0:T(8,128)S(1)} %bitcast.9), channel_id=1, replica_groups=mesh['pts'=16,'chip'=4,'core'=2] {'pts','chip'}, dimensions={0} | all-to-all | bytes 524288 | tf_op jit(solution)/shard_map/all_to_all | solution.py:244
  84.8 0.1 reduce_sum.9
  84.9 13.8 %all_to_all.17 = f32[64,8,128]{2,1,0:T(8,128)S(1)} all-to-all(f32[64,8,128]{2,1,0:T(8,128)S(1)} %broadcast_in_dim.2), channel_id=1, replica_groups=mesh['pts'=16,'chip'=4,'core'=2] {'pts','chip'}, dimensions={0} | all-to-all | bytes 524288 | tf_op jit(solution)/shard_map/all_to_all | solution.py:246
  98.7 3.0 %collective-permute-start.1 = (f32[32,2,8,128]{3,2,1,0:T(8,128)S(1)}, f32[32,2,8,128]{3,2,1,0:T(8,128)S(1)}, u32[]{:S(2)}, u32[]{:S(2)}) collective-permute-start(f32[32,2,8,128]{3,2,1,0:T(8,128)S(1)} %bitcast.5), channel_id=1, source_target_pairs={{0,1},{1,0},{2,3},{3,2},{4,5},{5,4},{6,7},{7,6},{8,9},{9,8},{10,11... | collective-permute-start | bytes 786440 | tf_op jit(solution)/shard_map/ppermute | solution.py:247
  101.7 0.4 own_gram.1.gram_ref
  102.1 0.7 collective-permute-done.1.other_ref
  102.9 8.0 %factor_and_apply.1 = (f32[256,2048]{1,0:T(8,128)}, f32[256,512]{1,0:T(8,128)}) custom-call(f32[256,256]{1,0:T(8,128)S(1)} %own_gram.1.gram_ref, f32[32,2,8,128]{3,2,1,0:T(8,128)S(1)} %bitcast.7, f32[32,2,8,128]{3,2,1,0:T(8,128)S(1)} %collective-permute-done.1.other_ref, f32[256,512]{1,0:T(8,128)S(1)} %copy-done, ...), custom_call_target="tpu_custom_call" | custom-call | tf_op jit(solution)/shard_map/factor_and_apply/pallas_call | solution.py:218
  (2 shorter events, 0.1 us)
Async XLA Ops:
  0.6 64.5 %copy-start = (f32[256,512]{1,0:T(8,128)S(1)}, f32[256,512]{1,0:T(8,128)}, u32[]{:S(2)}) copy-start(f32[256,512]{1,0:T(8,128)} %probes_ref.3) | copy-start | bytes 1572868
  68.8 2.2 %collective-permute-start = (f32[32,2,8,128]{3,2,1,0:T(8,128)S(1)}, f32[32,2,8,128]{3,2,1,0:T(8,128)S(1)}, u32[]{:S(2)}, u32[]{:S(2)}) collective-permute-start(f32[32,2,8,128]{3,2,1,0:T(8,128)S(1)} %get-tuple-element.7), channel_id=1, source_target_pairs={{0,1},{1,0},{2,3},{3,2},{4,5},{5,4},{6,7},{7,6},{8,9},{9,8},{10,11... | collective-permute-start | bytes 786440 | tf_op jit(solution)/shard_map/ppermute | solution.py:243
  98.7 4.2 %collective-permute-start.1 = (f32[32,2,8,128]{3,2,1,0:T(8,128)S(1)}, f32[32,2,8,128]{3,2,1,0:T(8,128)S(1)}, u32[]{:S(2)}, u32[]{:S(2)}) collective-permute-start(f32[32,2,8,128]{3,2,1,0:T(8,128)S(1)} %bitcast.5), channel_id=1, source_target_pairs={{0,1},{1,0},{2,3},{3,2},{4,5},{5,4},{6,7},{7,6},{8,9},{9,8},{10,11... | collective-permute-start | bytes 786440 | tf_op jit(solution)/shard_map/ppermute | solution.py:247

commit v9 on v8

--- a/solution.py
+++ b/solution.py
@@ -177,7 +177,24 @@
     )(own, probes)
 
 
-def factor_body(gram_ref, own_ref, other_ref, probes_ref, high_ref, low_ref, basis_ref, coeffs_ref, basis_out, coeffs_out, sems):
+def merge_body(high_ref, low_ref, whole_ref):
+    whole_ref[...] = high_ref[HALF:, :].astype(jnp.float32) + low_ref[HALF:, :].astype(jnp.float32)
+
+
+def merge_second(high, low):
+    k, pts = high.shape
+    vmem = pl.BlockSpec(memory_space=pltpu.VMEM)
+    return pl.pallas_call(
+        merge_body,
+        name="merge_second",
+        in_specs=[vmem, vmem],
+        out_specs=vmem,
+        out_shape=jax.ShapeDtypeStruct((k - HALF, pts), jnp.float32),
+        compiler_params=pltpu.CompilerParams(vmem_limit_bytes=32 << 20),
+    )(high, low)
+
+
+def factor_body(gram_ref, own_ref, other_ref, probes_ref, high_ref, low_ref, second_ref, basis_ref, coeffs_ref, basis_out, coeffs_out, sems):
     n = HALF
     k, pts = high_ref.shape
     own, other = join(own_ref), join(other_ref)
@@ -200,8 +217,7 @@
     write(basis_out, basis_ref, 0, 0, basis)
     coeffs = dot_split(upper, *split(moment[:n]))
     write(coeffs_out, coeffs_ref, 0, 0, coeffs)
-    second = high_ref[n:, :].astype(jnp.float32) + low_ref[n:, :].astype(jnp.float32)
-    high, low = split(second - dot_split(cross.T, *split(basis)))
+    high, low = split(second_ref[...] - dot_split(cross.T, *split(basis)))
     moment_high, moment_low = split(moment[n:] - dot_split(cross.T, *split(coeffs)))
     lower = inverse_factor(rest)
     for c in range(0, pts, pts // PIECES):
@@ -212,13 +228,13 @@
         copy.wait()
 
 
-def factor_and_apply(gram, own, other, probes, high, low):
+def factor_and_apply(gram, own, other, probes, high, low, second):
     k, pts = high.shape
     vmem = pl.BlockSpec(memory_space=pltpu.VMEM)
     return pl.pallas_call(
         factor_body,
         name="factor_and_apply",
-        in_specs=[vmem] * 6,
+        in_specs=[vmem] * 7,
         out_specs=[pl.BlockSpec(memory_space=pl.ANY), pl.BlockSpec(memory_space=pl.ANY)],
         out_shape=[
             jax.ShapeDtypeStruct((k, pts), jnp.float32),
@@ -230,7 +246,7 @@
             pltpu.SemaphoreType.DMA((PIECES + 3,)),
         ],
         compiler_params=pltpu.CompilerParams(vmem_limit_bytes=32 << 20),
-    )(gram, own, other, probes, high, low)
+    )(gram, own, other, probes, high, low, second)
 
 
 def on_device(fields, probes):
@@ -240,12 +256,13 @@
     sent = fields.reshape(per, devices, n_points // devices).transpose(1, 0, 2)
     panels = lax.all_to_all(sent, AXES, split_axis=0, concat_axis=0, tiled=True)
     high, low, own, other = sketch(panels, probes, 1.0 / n_points)
+    second = merge_second(high, low)
     parts = (own + lax.ppermute(other, "core", SWAP)).reshape(chips, -1, 128)
     parts = lax.all_to_all(parts, CHIPS, split_axis=0, concat_axis=0, tiled=True)
     total = jnp.broadcast_to(jnp.sum(parts, axis=0)[None], parts.shape)
     total = lax.all_to_all(total, CHIPS, split_axis=0, concat_axis=0, tiled=True).reshape(own.shape)
     swapped = lax.ppermute(total, "core", SWAP)
-    basis_rows, coeffs = factor_and_apply(own_gram(total, probes), total, swapped, probes, high, low)
+    basis_rows, coeffs = factor_and_apply(own_gram(total, probes), total, swapped, probes, high, low, second)
     return (basis_rows, coeffs)
 
 

time: 111 us -> 111 us (level)
    pallas_call x1 -> x2, Pallas kernels: 7.99 us -> 8.04 us  [the longest x1 7.93 us: factor_and_apply(): pl.pallas_call(factor_body, name='factor_and_apply', in_specs=[vmem] * 7,...]
where the time goes in v9:
time: 111 us
  blocking collectives  92.1 us (83%)
  Pallas kernels  12.1 us (11%)
  starting transfers between devices  4.07 us (4%)
  waiting for transfers between devices  1.79 us (2%)
    all_to_all x1, blocking collectives, on_device(): panels = lax.all_to_all(sent, AXES, split_axis=0, concat_axis=0, tiled=True)  64.5 us
    all_to_all x1, blocking collectives, on_device(): lax.all_to_all(parts, CHIPS, split_axis=0, concat_axis=0, tiled=True)  13.8 us
    all_to_all x1, blocking collectives, on_device(): lax.all_to_all(total, CHIPS, split_axis=0, concat_axis=0, tiled=True)  13.8 us
    pallas_call x1, Pallas kernels, factor_and_apply(): pl.pallas_call(factor_body, name='factor_and_apply', in_specs=[vmem] * 7,...  7.93 us
    pallas_call x1, Pallas kernels, sketch(): pl.pallas_call(lambda *refs: sketch_body(scale, *refs), name='sketch', in...  3.6 us
    ppermute x1, starting transfers between devices, on_device(): swapped = lax.ppermute(total, 'core', SWAP)  3.05 us
  transfers between devices with their start and end apart: 2, of which 2 were waited for; matrix products, arithmetic and copies ran while one was open for 0% of the time, Pallas kernels for 0%

profile of v9, /device:TPU:1, one launch (start us, length us, event | category | flops | bytes accessed | tf_op | source)
XLA Modules:
  0.0 111.0 jit_solution(8313209276044772314)
XLA Ops:
  0.6 0.0 copy-start
  0.6 64.5 %all_to_all.15.refs_0_ = f32[128,4,2048]{2,1,0:T(4,128)S(1)} all-to-all(f32[128,4,2048]{2,1,0:T(4,128)} %bitcast.8), channel_id=1, replica_groups=mesh['pts'=16,'chip'=4,'core'=2] {'pts','chip','core'}, dimensions={0} | all-to-all | bytes 8388608 | tf_op jit(solution)/shard_map/all_to_all | solution.py:257
  65.1 0.0 copy-done
  65.1 3.6 %sketch.1 = (bf16[256,2048]{1,0:T(8,128)(2,1)S(1)}, bf16[256,2048]{1,0:T(8,128)(2,1)S(1)}, f32[32,2,8,128]{3,2,1,0:T(8,128)S(1)}, f32[32,2,8,128]{3,2,1,0:T(8,128)S(1)}) custom-call(f32[128,4,2048]{2,1,0:T(4,128)S(1)} %all_to_all.15.refs_0_, f32[256,512]{1,0:T(8,128)S(1)} %copy-done), custom_call_target="tpu_custom_call" | custom-call | tf_op jit(solution)/shard_map/sketch/pallas_call | solution.py:83
  68.8 1.0 collective-permute-start
  69.8 1.2 %collective-permute-done = f32[32,2,8,128]{3,2,1,0:T(8,128)S(1)} collective-permute-done((f32[32,2,8,128]{3,2,1,0:T(8,128)S(1)}, f32[32,2,8,128]{3,2,1,0:T(8,128)S(1)}, u32[]{:S(2)}, u32[]{:S(2)}) %collective-permute-start) | collective-permute-done | bytes 262176 | tf_op jit(solution)/shard_map/ppermute | solution.py:260
  71.0 13.8 %all_to_all.16 = f32[64,8,128]{2,1,0:T(8,128)S(1)} all-to-all(f32[64,8,128]{2,1,0:T(8,128)S(1)} %bitcast.9), channel_id=1, replica_groups=mesh['pts'=16,'chip'=4,'core'=2] {'pts','chip'}, dimensions={0} | all-to-all | bytes 524288 | tf_op jit(solution)/shard_map/all_to_all | solution.py:261
  84.8 0.1 reduce_sum.9
  84.9 13.8 %all_to_all.17 = f32[64,8,128]{2,1,0:T(8,128)S(1)} all-to-all(f32[64,8,128]{2,1,0:T(8,128)S(1)} %broadcast_in_dim.2), channel_id=1, replica_groups=mesh['pts'=16,'chip'=4,'core'=2] {'pts','chip'}, dimensions={0} | all-to-all | bytes 524288 | tf_op jit(solution)/shard_map/all_to_all | solution.py:263
  98.7 3.0 %collective-permute-start.1 = (f32[32,2,8,128]{3,2,1,0:T(8,128)S(1)}, f32[32,2,8,128]{3,2,1,0:T(8,128)S(1)}, u32[]{:S(2)}, u32[]{:S(2)}) collective-permute-start(f32[32,2,8,128]{3,2,1,0:T(8,128)S(1)} %bitcast.5), channel_id=1, source_target_pairs={{0,1},{1,0},{2,3},{3,2},{4,5},{5,4},{6,7},{7,6},{8,9},{9,8},{10,11... | collective-permute-start | bytes 786440 | tf_op jit(solution)/shard_map/ppermute | solution.py:264
  101.7 0.1 merge_second.1.second_ref
  101.8 0.4 own_gram.1.gram_ref
  102.3 0.6 collective-permute-done.1.other_ref
  102.9 7.9 %factor_and_apply.1 = (f32[256,2048]{1,0:T(8,128)}, f32[256,512]{1,0:T(8,128)}) custom-call(f32[256,256]{1,0:T(8,128)S(1)} %own_gram.1.gram_ref, f32[32,2,8,128]{3,2,1,0:T(8,128)S(1)} %bitcast.7, f32[32,2,8,128]{3,2,1,0:T(8,128)S(1)} %collective-permute-done.1.other_ref, f32[256,512]{1,0:T(8,128)S(1)} %copy-done, ...), custom_call_target="tpu_custom_call" | custom-call | tf_op jit(solution)/shard_map/factor_and_apply/pallas_call | solution.py:234
  (2 shorter events, 0.1 us)
Async XLA Ops:
  0.6 64.5 %copy-start = (f32[256,512]{1,0:T(8,128)S(1)}, f32[256,512]{1,0:T(8,128)}, u32[]{:S(2)}) copy-start(f32[256,512]{1,0:T(8,128)} %probes_ref.3) | copy-start | bytes 1572868
  68.8 2.2 %collective-permute-start = (f32[32,2,8,128]{3,2,1,0:T(8,128)S(1)}, f32[32,2,8,128]{3,2,1,0:T(8,128)S(1)}, u32[]{:S(2)}, u32[]{:S(2)}) collective-permute-start(f32[32,2,8,128]{3,2,1,0:T(8,128)S(1)} %get-tuple-element.7), channel_id=1, source_target_pairs={{0,1},{1,0},{2,3},{3,2},{4,5},{5,4},{6,7},{7,6},{8,9},{9,8},{10,11... | collective-permute-start | bytes 786440 | tf_op jit(solution)/shard_map/ppermute | solution.py:260
  98.7 4.2 %collective-permute-start.1 = (f32[32,2,8,128]{3,2,1,0:T(8,128)S(1)}, f32[32,2,8,128]{3,2,1,0:T(8,128)S(1)}, u32[]{:S(2)}, u32[]{:S(2)}) collective-permute-start(f32[32,2,8,128]{3,2,1,0:T(8,128)S(1)} %bitcast.5), channel_id=1, source_target_pairs={{0,1},{1,0},{2,3},{3,2},{4,5},{5,4},{6,7},{7,6},{8,9},{9,8},{10,11... | collective-permute-start | bytes 786440 | tf_op jit(solution)/shard_map/ppermute | solution.py:264
